TPU v7x, 512 devices: a whole 4x4x16 slice. The times are simulated.
512 devices in a mesh: frames: 128 (over z, x, core), heads: 4 (over y).
Axes of the slice: x: 4, y: 4, z: 16, core: 2. Of those that a mesh axis runs over, the one named last changes fastest.
Arguments:
- query_states: bfloat16 [256, 128, 1024], P('frames', 'heads'), may hold values from -6 to 6
- key_states: bfloat16 [256, 128, 1024], P('frames', 'heads'), may hold values from -6 to 6
- value_states: bfloat16 [256, 128, 1024], P('frames', 'heads'), may hold values from -6 to 6
- out_grad: bfloat16 [256, 128, 1024], P('frames', 'heads'), may hold values from -6 to 6
- partners: int32 [256, 6], replicated, may hold values from -1 to 255, as said below
Outputs:
- attended: bfloat16 [256, 128, 1024], P('frames', 'heads')
- query_grad: bfloat16 [256, 128, 1024], P('frames', 'heads')
- key_grad: bfloat16 [256, 128, 1024], P('frames', 'heads')
- value_grad: bfloat16 [256, 128, 1024], P('frames', 'heads')
Inputs may be any that keep to these rules, and one draw needn't show every extreme that they name: `partners`: row f lists the frames that frame f attends to besides itself: distinct frames g other than f with |g - f| <= 6, followed by -1 in the unused slots. Every row lists at least one frame. In every draw some aligned group of 2 frames (k * 2 to k * 2 + 1) uses all 6 slots in each of its rows.
All inputs are finite; a program needn't handle non-finite values.
Results may differ from a plain program's by a relative error of at most 0.024.
Values may be sent and summed in bfloat16 or wider, within the bound.
A program may use at most 64 MiB of HBM per device.

v0:
```python
import jax
import jax.numpy as jnp
from jax import lax
from jax.sharding import PartitionSpec as P

HEAD_DIM = 64
REACH = 3
WINDOW = 6


def passed_along(value, axis, steps):
    count = lax.axis_size(axis)
    leading, last = (max(0, -steps), min(count, count - steps))
    return lax.ppermute(value, axis, [(source, source + steps) for source in range(leading, last)])


def in_one_piece(arrays, axis, split_dim, concat_dim, along):
    both = jnp.concatenate(arrays, axis=along)
    result, at, finished = (
        lax.all_to_all(both, axis, split_axis=split_dim, concat_axis=concat_dim, tiled=True),
        0,
        [],
    )
    for a in arrays:
        finished.append(lax.slice_in_dim(result, at, at + a.shape[along], axis=along))
        at += a.shape[along]
    return tuple(finished)


def window_shift(stacked, offset):
    return passed_along(stacked, "frames", offset)


def return_shift(stacked, offset):
    return passed_along(stacked, "frames", offset)


def attend(query, grad_out, win_keys, win_values, partners, first):
    frame_count, token_count, width = query.shape
    head_count = width // HEAD_DIM
    span = win_keys.shape[0]
    scale = float(HEAD_DIM) ** (-0.5)
    highest = lax.Precision.HIGHEST
    slot_count = partners.shape[1] + 1
    own_partners = lax.dynamic_slice_in_dim(partners, first, frame_count, 0)
    local = jnp.arange(frame_count, dtype=jnp.int32)
    centre = (local + WINDOW)[:, None]
    present = jnp.concatenate([jnp.ones((frame_count, 1), jnp.bool_), own_partners >= 0], axis=1)
    listed = jnp.concatenate([centre, own_partners - first + WINDOW], axis=1)
    index = jnp.where(present, listed, centre)
    flat_index = index.T.reshape(-1)
    tile_shape = (slot_count, frame_count, token_count, head_count, HEAD_DIM)
    slot_keys = jnp.take(win_keys, flat_index, axis=0).reshape(tile_shape)
    slot_values = jnp.take(win_values, flat_index, axis=0).reshape(tile_shape)
    query_four = query.reshape(frame_count, token_count, head_count, HEAD_DIM)
    grad_four = grad_out.reshape(frame_count, token_count, head_count, HEAD_DIM)
    columns = jnp.arange(span, dtype=jnp.int32)

    def scores_of(slot):
        scores = (
            jnp.einsum(
                "aqhd,akhd->ahqk", query_four, slot_keys[slot], preferred_element_type=jnp.float32
            )
            * scale
        )
        return jnp.where(present[:, slot, None, None, None], scores, -jnp.inf)

    scores = scores_of(0)
    peak = jnp.max(scores, axis=3)
    total = jnp.sum(jnp.exp(scores - peak[..., None]), axis=3)
    for slot in range(1, slot_count):
        scores = scores_of(slot)
        new_peak = jnp.maximum(peak, jnp.max(scores, axis=3))
        total = total * jnp.exp(peak - new_peak) + jnp.sum(
            jnp.exp(scores - new_peak[..., None]), axis=3
        )
        peak = new_peak
    logsum = peak + jnp.log(total)
    mixed = jnp.zeros((frame_count, token_count, head_count, HEAD_DIM), jnp.float32)
    for slot in range(slot_count):
        rounded = jnp.exp(scores_of(slot) - logsum[..., None]).astype(jnp.bfloat16)
        mixed = mixed + jnp.einsum(
            "ahqk,akhd->aqhd", rounded, slot_values[slot], preferred_element_type=jnp.float32
        )
    attended = mixed.reshape(frame_count, token_count, width).astype(jnp.bfloat16)
    product = grad_out.astype(jnp.float32) * attended.astype(jnp.float32)
    delta = jnp.sum(
        product.reshape(frame_count, token_count, head_count, HEAD_DIM), axis=3
    ).transpose(0, 2, 1)
    query_sum = jnp.zeros((frame_count, token_count, head_count, HEAD_DIM), jnp.float32)
    key_list = []
    value_list = []
    for slot in range(slot_count):
        weights = jnp.exp(scores_of(slot) - logsum[..., None])
        rounded = weights.astype(jnp.bfloat16)
        prob_grad = jnp.einsum(
            "aqhd,akhd->ahqk", grad_four, slot_values[slot], preferred_element_type=jnp.float32
        )
        score_grad = (weights * (prob_grad - delta[..., None])).astype(jnp.bfloat16)
        query_sum = (
            query_sum
            + jnp.einsum(
                "ahqk,akhd->aqhd", score_grad, slot_keys[slot], preferred_element_type=jnp.float32
            )
            * scale
        )
        key_list.append(
            jnp.einsum(
                "ahqk,aqhd->akhd", score_grad, query_four, preferred_element_type=jnp.float32
            )
            * scale
        )
        value_list.append(
            jnp.einsum("ahqk,aqhd->akhd", rounded, grad_four, preferred_element_type=jnp.float32)
        )
    placing = ((index.T[:, :, None] == columns[None, None, :]) & present.T[:, :, None]).astype(
        jnp.float32
    )
    key_terms = jnp.stack(key_list).reshape(slot_count, frame_count, token_count * width)
    value_terms = jnp.stack(value_list).reshape(slot_count, frame_count, token_count * width)
    key_sum = jnp.einsum("saw,sam->wm", placing, key_terms, precision=highest)
    value_sum = jnp.einsum("saw,sam->wm", placing, value_terms, precision=highest)
    query_grad = query_sum.reshape(frame_count, token_count, width)
    key_sum = key_sum.reshape(span, token_count, width)
    value_sum = value_sum.reshape(span, token_count, width)
    return (attended, query_grad, key_sum, value_sum)


def per_device(query_states, key_states, value_states, out_grad, partners):
    query, keyed, valued, grad_out = in_one_piece(
        (query_states, key_states, value_states, out_grad), "heads", 2, 1, 0
    )
    own_frames = query.shape[0]
    first = lax.axis_index("frames") * own_frames
    stacked = jnp.stack((keyed, valued))
    lower = []
    upper = []
    for step in range(1, REACH + 1):
        lower.append(window_shift(stacked, step))
        upper.append(window_shift(stacked, -step))
    pieces = lower[::-1] + [stacked] + upper
    win_keys = jnp.concatenate([piece[0] for piece in pieces], axis=0)
    win_values = jnp.concatenate([piece[1] for piece in pieces], axis=0)
    attended, query_grad, key_sum, value_sum = attend(
        query, grad_out, win_keys, win_values, partners, first
    )
    own_key = key_sum[WINDOW : WINDOW + own_frames]
    own_value = value_sum[WINDOW : WINDOW + own_frames]
    for step in range(1, REACH + 1):
        below = (REACH - step) * own_frames
        arrived = return_shift(
            jnp.stack((key_sum[below : below + own_frames], value_sum[below : below + own_frames])),
            -step,
        )
        own_key = own_key + arrived[0]
        own_value = own_value + arrived[1]
        above = (REACH + step) * own_frames
        arrived = return_shift(
            jnp.stack((key_sum[above : above + own_frames], value_sum[above : above + own_frames])),
            step,
        )
        own_key = own_key + arrived[0]
        own_value = own_value + arrived[1]
    query_grad = query_grad.astype(jnp.bfloat16)
    key_grad = own_key.astype(jnp.bfloat16)
    value_grad = own_value.astype(jnp.bfloat16)
    return in_one_piece((attended, query_grad, key_grad, value_grad), "heads", 1, 2, 0)


def solution(mesh):
    return jax.shard_map(
        per_device,
        mesh=mesh,
        in_specs=(
            P("frames", "heads", None),
            P("frames", "heads", None),
            P("frames", "heads", None),
            P("frames", "heads", None),
            P(),
        ),
        out_specs=(
            P("frames", "heads", None),
            P("frames", "heads", None),
            P("frames", "heads", None),
            P("frames", "heads", None),
        ),
        check_vma=False,
    )
```

profile of v0, /device:TPU:135, one launch (start us, length us, event | category | flops | bytes accessed | tf_op | source)
XLA Modules:
  0.0 184.1 jit_solution(17892315868930555991)
XLA Ops:
  0.6 1.2 pad_maximum_fusion
  1.8 1.6 copy.432
  3.5 2.9 %reshape.287 = bf16[4,2,32768]{2,1,0:T(2,128)(2,1)} reshape(bf16[1024,8,32]{2,1,0:T(8,128)(2,1)S(1)} %bitcast.331) | data formatting | bytes 1048576
  6.4 4.2 %all-to-all-start = ((bf16[4,2,32768]{2,1,0:T(2,128)(2,1)}), bf16[4,2,32768]{2,1,0:T(2,128)(2,1)S(1)}, u32[]{:S(2)}, u32[]{:S(2)}) async-start(bf16[4,2,32768]{2,1,0:T(2,128)(2,1)} %reshape.287), calls=%async_computation | async-start | bytes 1048576 | tf_op jit(solution)/shard_map/all_to_all | solution.py:20
  11.4 7.5 %all-to-all-done = bf16[4,2,32768]{2,1,0:T(2,128)(2,1)S(1)} async-done(((bf16[4,2,32768]{2,1,0:T(2,128)(2,1)}), bf16[4,2,32768]{2,1,0:T(2,128)(2,1)S(1)}, u32[]{:S(2)}, u32[]{:S(2)}) %all-to-all-start) | async-done | bytes 524320 | tf_op jit(solution)/shard_map/all_to_all | solution.py:20
  18.9 1.1 reshape.288
  20.0 1.6 copy.604
  21.9 6.4 %collective-permute-start = (bf16[2,2,128,256]{3,2,1,0:T(8,128)(2,1)S(1)}, bf16[2,2,128,256]{3,2,1,0:T(8,128)(2,1)S(1)}, u32[]{:S(2)}, u32[]{:S(2)}) collective-permute-start(bf16[2,2,128,256]{3,2,1,0:T(8,128)(2,1)S(1)} %pad_maximum_fusion.8), channel_id=1, source_target_pairs={{0,12},{4,16},{8,20},{12,24},{16,28},{20,32},{24,36},{28,40},{32,4... | collective-permute-start | bytes 786440 | tf_op jit(solution)/shard_map/ppermute | solution.py:14
  28.8 3.7 %collective-permute-start.1 = (bf16[2,2,128,256]{3,2,1,0:T(8,128)(2,1)S(1)}, bf16[2,2,128,256]{3,2,1,0:T(8,128)(2,1)}, u32[]{:S(2)}, u32[]{:S(2)}) collective-permute-start(bf16[2,2,128,256]{3,2,1,0:T(8,128)(2,1)S(1)} %pad_maximum_fusion.8), channel_id=1, source_target_pairs={{0,8},{4,12},{8,16},{12,20},{16,24},{20,28},{24,32},{28,36},{32,40... | collective-permute-start | bytes 786440 | tf_op jit(solution)/shard_map/ppermute | solution.py:14
  32.7 1.9 %collective-permute-start.2 = (bf16[2,2,128,256]{3,2,1,0:T(8,128)(2,1)S(1)}, bf16[2,2,128,256]{3,2,1,0:T(8,128)(2,1)}, u32[]{:S(2)}, u32[]{:S(2)}) collective-permute-start(bf16[2,2,128,256]{3,2,1,0:T(8,128)(2,1)S(1)} %pad_maximum_fusion.8), channel_id=1, source_target_pairs={{0,4},{4,8},{8,12},{12,16},{16,20},{20,24},{24,28},{28,32},{32,36}... | collective-permute-start | bytes 786440 | tf_op jit(solution)/shard_map/ppermute | solution.py:14
  34.6 2.4 %collective-permute-start.3 = (bf16[2,2,128,256]{3,2,1,0:T(8,128)(2,1)S(1)}, bf16[2,2,128,256]{3,2,1,0:T(8,128)(2,1)S(1)}, u32[]{:S(2)}, u32[]{:S(2)}) collective-permute-start(bf16[2,2,128,256]{3,2,1,0:T(8,128)(2,1)S(1)} %pad_maximum_fusion.8), channel_id=1, source_target_pairs={{4,0},{8,4},{12,8},{16,12},{20,16},{24,20},{28,24},{32,28},{36,32}... | collective-permute-start | bytes 786440 | tf_op jit(solution)/shard_map/ppermute | solution.py:14
  37.1 1.9 %collective-permute-start.4 = (bf16[2,2,128,256]{3,2,1,0:T(8,128)(2,1)S(1)}, bf16[2,2,128,256]{3,2,1,0:T(8,128)(2,1)S(1)}, u32[]{:S(2)}, u32[]{:S(2)}) collective-permute-start(bf16[2,2,128,256]{3,2,1,0:T(8,128)(2,1)S(1)} %pad_maximum_fusion.8), channel_id=1, source_target_pairs={{8,0},{12,4},{16,8},{20,12},{24,16},{28,20},{32,24},{36,28},{40,32... | collective-permute-start | bytes 786440 | tf_op jit(solution)/shard_map/ppermute | solution.py:14
  39.7 2.1 %collective-permute-start.5 = (bf16[2,2,128,256]{3,2,1,0:T(8,128)(2,1)S(1)}, bf16[2,2,128,256]{3,2,1,0:T(8,128)(2,1)S(1)}, u32[]{:S(2)}, u32[]{:S(2)}) collective-permute-start(bf16[2,2,128,256]{3,2,1,0:T(8,128)(2,1)S(1)} %pad_maximum_fusion.8), channel_id=1, source_target_pairs={{12,0},{16,4},{20,8},{24,12},{28,16},{32,20},{36,24},{40,28},{44,3... | collective-permute-start | bytes 786440 | tf_op jit(solution)/shard_map/ppermute | solution.py:14
  43.9 1.5 collective-permute-done.3
  45.4 5.2 %collective-permute-done.4 = bf16[2,2,128,256]{3,2,1,0:T(8,128)(2,1)S(1)} collective-permute-done((bf16[2,2,128,256]{3,2,1,0:T(8,128)(2,1)S(1)}, bf16[2,2,128,256]{3,2,1,0:T(8,128)(2,1)S(1)}, u32[]{:S(2)}, u32[]{:S(2)}) %collective-permute-start.4) | collective-permute-done | bytes 262176 | tf_op jit(solution)/shard_map/ppermute | solution.py:14
  50.6 2.3 %collective-permute-done.5 = bf16[2,2,128,256]{3,2,1,0:T(8,128)(2,1)S(1)} collective-permute-done((bf16[2,2,128,256]{3,2,1,0:T(8,128)(2,1)S(1)}, bf16[2,2,128,256]{3,2,1,0:T(8,128)(2,1)S(1)}, u32[]{:S(2)}, u32[]{:S(2)}) %collective-permute-start.5) | collective-permute-done | bytes 262176 | tf_op jit(solution)/shard_map/ppermute | solution.py:14
  72.9 1.2 stack.154
  74.7 1.2 stack.153
  76.4 1.2 stack.152
  78.1 1.2 stack.151
  79.8 1.4 stack.150
  81.5 1.2 stack.149
  82.9 1.2 stack.148
  84.1 5.2 %stack.121 = f32[7,2,32768]{2,0,1:T(8,128)S(1)} concatenate(f32[1,2,32768]{2,0,1:T(1,128)} %stack.148, f32[1,2,32768]{2,0,1:T(1,128)} %stack.149, f32[1,2,32768]{2,0,1:T(1,128)} %stack.150, f32[1,2,32768]{2,0,1:T(1,128)} %stack.151, f32[1,2,32768]{2,0,1:T(1,128)} %stack.152, f32[1,2,32768]{2,0,1:T(1,128)} %stack.153, f32[1,2,32768]{2,0,1:T(1,128)} %stack.154), dimensions={0} | concatenate | bytes 3670016 | tf_op jit(solution)/shard_map/stack | solution.py:119
  89.2 1.5 convolution_bitcast_fusion.1
  90.8 1.5 fusion.87
  92.6 1.2 stack.161
  94.0 1.2 stack.160
  95.4 1.2 stack.159
  96.9 1.2 stack.158
  98.3 1.2 stack.157
  99.8 1.2 stack.156
  101.2 1.2 stack.155
  102.4 5.2 %stack.130 = f32[7,2,32768]{2,0,1:T(8,128)S(1)} concatenate(f32[1,2,32768]{2,0,1:T(1,128)} %stack.155, f32[1,2,32768]{2,0,1:T(1,128)} %stack.156, f32[1,2,32768]{2,0,1:T(1,128)} %stack.157, f32[1,2,32768]{2,0,1:T(1,128)} %stack.158, f32[1,2,32768]{2,0,1:T(1,128)} %stack.159, f32[1,2,32768]{2,0,1:T(1,128)} %stack.160, f32[1,2,32768]{2,0,1:T(1,128)} %stack.161), dimensions={0} | concatenate | bytes 3670016 | tf_op jit(solution)/shard_map/stack | solution.py:120
  107.6 1.5 convolution_bitcast_fusion
  110.3 7.0 %collective-permute-start.6 = (f32[2,2,128,256]{3,1,2,0:T(2,128)S(1)}, f32[2,2,128,256]{3,1,2,0:T(2,128)S(1)}, u32[]{:S(2)}, u32[]{:S(2)}) collective-permute-start(f32[2,2,128,256]{3,1,2,0:T(2,128)S(1)} %pad_maximum_fusion.1), channel_id=1, source_target_pairs={{4,0},{8,4},{12,8},{16,12},{20,16},{24,20},{28,24},{32,28},{36,32}... | collective-permute-start | bytes 1572872 | tf_op jit(solution)/shard_map/ppermute | solution.py:14
  117.3 1.1 pad_maximum_fusion.2
  118.4 2.3 %collective-permute-start.7 = (f32[2,2,128,256]{3,1,2,0:T(2,128)}, f32[2,2,128,256]{3,1,2,0:T(2,128)S(1)}, u32[]{:S(2)}, u32[]{:S(2)}) collective-permute-start(f32[2,2,128,256]{3,1,2,0:T(2,128)} %pad_maximum_fusion.2), channel_id=1, source_target_pairs={{0,4},{4,8},{8,12},{12,16},{16,20},{20,24},{24,28},{28,32},{32,36}... | collective-permute-start | bytes 1572872 | tf_op jit(solution)/shard_map/ppermute | solution.py:14
  121.8 4.5 %collective-permute-start.8 = (f32[2,2,128,256]{3,1,2,0:T(2,128)}, f32[2,2,128,256]{3,1,2,0:T(2,128)S(1)}, u32[]{:S(2)}, u32[]{:S(2)}) collective-permute-start(f32[2,2,128,256]{3,1,2,0:T(2,128)} %pad_maximum_fusion.3), channel_id=1, source_target_pairs={{8,0},{12,4},{16,8},{20,12},{24,16},{28,20},{32,24},{36,28},{40,32... | collective-permute-start | bytes 1572872 | tf_op jit(solution)/shard_map/ppermute | solution.py:14
  126.3 1.0 pad_maximum_fusion.4
  127.3 3.1 %collective-permute-start.9 = (f32[2,2,128,256]{3,1,2,0:T(2,128)}, f32[2,2,128,256]{3,1,2,0:T(2,128)}, u32[]{:S(2)}, u32[]{:S(2)}) collective-permute-start(f32[2,2,128,256]{3,1,2,0:T(2,128)} %pad_maximum_fusion.4), channel_id=1, source_target_pairs={{0,8},{4,12},{8,16},{12,20},{16,24},{20,28},{24,32},{28,36},{32,40... | collective-permute-start | bytes 1572872 | tf_op jit(solution)/shard_map/ppermute | solution.py:14
  131.5 1.9 %collective-permute-start.10 = (f32[2,2,128,256]{3,1,2,0:T(2,128)}, f32[2,2,128,256]{3,1,2,0:T(2,128)}, u32[]{:S(2)}, u32[]{:S(2)}) collective-permute-start(f32[2,2,128,256]{3,1,2,0:T(2,128)} %pad_maximum_fusion.5), channel_id=1, source_target_pairs={{12,0},{16,4},{20,8},{24,12},{28,16},{32,20},{36,24},{40,28},{44,3... | collective-permute-start | bytes 1572872 | tf_op jit(solution)/shard_map/ppermute | solution.py:14
  134.9 6.2 %collective-permute-start.11 = (f32[2,2,128,256]{3,1,2,0:T(2,128)}, f32[2,2,128,256]{3,1,2,0:T(2,128)}, u32[]{:S(2)}, u32[]{:S(2)}) collective-permute-start(f32[2,2,128,256]{3,1,2,0:T(2,128)} %pad_maximum_fusion.6), channel_id=1, source_target_pairs={{0,12},{4,16},{8,20},{12,24},{16,28},{20,32},{24,36},{28,40},{32,4... | collective-permute-start | bytes 1572872 | tf_op jit(solution)/shard_map/ppermute | solution.py:14
  142.1 1.5 collective-permute-done.9
  143.6 6.2 %collective-permute-done.10 = f32[2,2,128,256]{3,1,2,0:T(2,128)} collective-permute-done((f32[2,2,128,256]{3,1,2,0:T(2,128)}, f32[2,2,128,256]{3,1,2,0:T(2,128)}, u32[]{:S(2)}, u32[]{:S(2)}) %collective-permute-start.10) | collective-permute-done | bytes 524320 | tf_op jit(solution)/shard_map/ppermute | solution.py:14
  149.8 19.4 %collective-permute-done.11 = f32[2,2,128,256]{3,1,2,0:T(2,128)} collective-permute-done((f32[2,2,128,256]{3,1,2,0:T(2,128)}, f32[2,2,128,256]{3,1,2,0:T(2,128)}, u32[]{:S(2)}, u32[]{:S(2)}) %collective-permute-start.11) | collective-permute-done | bytes 524320 | tf_op jit(solution)/shard_map/ppermute | solution.py:14
  169.3 2.1 %fusion.45 = (bf16[2,128,256]{2,0,1:T(2,128)(2,1)S(1)}, bf16[2,128,256]{2,0,1:T(2,128)(2,1)S(1)}) fusion(f32[2,2,128,256]{3,1,2,0:T(2,128)} %collective-permute-done.11, f32[2,2,128,256]{3,1,2,0:T(2,128)} %collective-permute-done.10, f32[2,2,128,256]{3,1,2,0:T(2,128)} %collective-permute-done.9, f32[2,2,128,256]{3,1,2,0:T(2,128)S(1)} %collective-permute-done.8, ...), kind=kLoop, calls=%fused_computation.120 | loop fusion | flops 917504 | bytes 3932160 | tf_op jit(solution)/shard_map/convert_element_type | solution.py:165
  171.9 9.3 %all_to_all.30 = bf16[8,128,256]{2,0,1:T(8,128)(2,1)S(1)} all-to-all(bf16[8,128,256]{2,0,1:T(8,128)(2,1)S(1)} %pad_maximum_fusion.7), channel_id=1, replica_groups=mesh['frames'=128,'heads'=4] {'heads'}, dimensions={1} | all-to-all | bytes 1048576 | tf_op jit(solution)/shard_map/all_to_all | solution.py:20
  (200 shorter events, 37.3 us)
Async XLA Ops:
  3.4 7.1 %copy-start.26 = (s32[256,6]{0,1:T(8,128)S(1)}, s32[256,6]{0,1:T(8,128)}, u32[]{:S(2)}) copy-start(s32[256,6]{0,1:T(8,128)} %param.11) | copy-start | bytes 18436
  6.4 12.5 %all-to-all-start = ((bf16[4,2,32768]{2,1,0:T(2,128)(2,1)}), bf16[4,2,32768]{2,1,0:T(2,128)(2,1)S(1)}, u32[]{:S(2)}, u32[]{:S(2)}) async-start(bf16[4,2,32768]{2,1,0:T(2,128)(2,1)} %reshape.287), calls=%async_computation | async-start | bytes 1048576 | tf_op jit(solution)/shard_map/all_to_all | solution.py:20
  21.9 17.8 %collective-permute-start = (bf16[2,2,128,256]{3,2,1,0:T(8,128)(2,1)S(1)}, bf16[2,2,128,256]{3,2,1,0:T(8,128)(2,1)S(1)}, u32[]{:S(2)}, u32[]{:S(2)}) collective-permute-start(bf16[2,2,128,256]{3,2,1,0:T(8,128)(2,1)S(1)} %pad_maximum_fusion.8), channel_id=1, source_target_pairs={{0,12},{4,16},{8,20},{12,24},{16,28},{20,32},{24,36},{28,40},{32,4... | collective-permute-start | bytes 786440 | tf_op jit(solution)/shard_map/ppermute | solution.py:14
  28.8 13.1 %collective-permute-start.1 = (bf16[2,2,128,256]{3,2,1,0:T(8,128)(2,1)S(1)}, bf16[2,2,128,256]{3,2,1,0:T(8,128)(2,1)}, u32[]{:S(2)}, u32[]{:S(2)}) collective-permute-start(bf16[2,2,128,256]{3,2,1,0:T(8,128)(2,1)S(1)} %pad_maximum_fusion.8), channel_id=1, source_target_pairs={{0,8},{4,12},{8,16},{12,20},{16,24},{20,28},{24,32},{28,36},{32,40... | collective-permute-start | bytes 786440 | tf_op jit(solution)/shard_map/ppermute | solution.py:14
  32.7 10.1 %collective-permute-start.2 = (bf16[2,2,128,256]{3,2,1,0:T(8,128)(2,1)S(1)}, bf16[2,2,128,256]{3,2,1,0:T(8,128)(2,1)}, u32[]{:S(2)}, u32[]{:S(2)}) collective-permute-start(bf16[2,2,128,256]{3,2,1,0:T(8,128)(2,1)S(1)} %pad_maximum_fusion.8), channel_id=1, source_target_pairs={{0,4},{4,8},{8,12},{12,16},{16,20},{20,24},{24,28},{28,32},{32,36}... | collective-permute-start | bytes 786440 | tf_op jit(solution)/shard_map/ppermute | solution.py:14
  34.6 10.8 %collective-permute-start.3 = (bf16[2,2,128,256]{3,2,1,0:T(8,128)(2,1)S(1)}, bf16[2,2,128,256]{3,2,1,0:T(8,128)(2,1)S(1)}, u32[]{:S(2)}, u32[]{:S(2)}) collective-permute-start(bf16[2,2,128,256]{3,2,1,0:T(8,128)(2,1)S(1)} %pad_maximum_fusion.8), channel_id=1, source_target_pairs={{4,0},{8,4},{12,8},{16,12},{20,16},{24,20},{28,24},{32,28},{36,32}... | collective-permute-start | bytes 786440 | tf_op jit(solution)/shard_map/ppermute | solution.py:14
  37.1 13.5 %collective-permute-start.4 = (bf16[2,2,128,256]{3,2,1,0:T(8,128)(2,1)S(1)}, bf16[2,2,128,256]{3,2,1,0:T(8,128)(2,1)S(1)}, u32[]{:S(2)}, u32[]{:S(2)}) collective-permute-start(bf16[2,2,128,256]{3,2,1,0:T(8,128)(2,1)S(1)} %pad_maximum_fusion.8), channel_id=1, source_target_pairs={{8,0},{12,4},{16,8},{20,12},{24,16},{28,20},{32,24},{36,28},{40,32... | collective-permute-start | bytes 786440 | tf_op jit(solution)/shard_map/ppermute | solution.py:14
  39.7 13.2 %collective-permute-start.5 = (bf16[2,2,128,256]{3,2,1,0:T(8,128)(2,1)S(1)}, bf16[2,2,128,256]{3,2,1,0:T(8,128)(2,1)S(1)}, u32[]{:S(2)}, u32[]{:S(2)}) collective-permute-start(bf16[2,2,128,256]{3,2,1,0:T(8,128)(2,1)S(1)} %pad_maximum_fusion.8), channel_id=1, source_target_pairs={{12,0},{16,4},{20,8},{24,12},{28,16},{32,20},{36,24},{40,28},{44,3... | collective-permute-start | bytes 786440 | tf_op jit(solution)/shard_map/ppermute | solution.py:14
  52.9 1.3 copy-start.32
  54.9 2.3 %copy-start.4 = (bf16[2,128,256]{1,2,0:T(8,128)(2,1)}, bf16[2,128,256]{1,2,0:T(8,128)(2,1)S(1)}, u32[]{:S(2)}) copy-start(bf16[2,128,256]{1,2,0:T(8,128)(2,1)S(1)} %copy.444) | copy-start | bytes 393220
  55.0 2.5 %copy-start.2 = (bf16[2,128,256]{1,2,0:T(8,128)(2,1)}, bf16[2,128,256]{1,2,0:T(8,128)(2,1)S(1)}, u32[]{:S(2)}) copy-start(bf16[2,128,256]{1,2,0:T(8,128)(2,1)S(1)} %copy.446) | copy-start | bytes 393220
  55.2 2.6 %copy-start = (bf16[2,128,256]{1,2,0:T(8,128)(2,1)}, bf16[2,128,256]{1,2,0:T(8,128)(2,1)S(1)}, u32[]{:S(2)}) copy-start(bf16[2,128,256]{1,2,0:T(8,128)(2,1)S(1)} %copy.448) | copy-start | bytes 393220
  55.4 3.0 %copy-start.6 = (bf16[2,128,256]{1,2,0:T(8,128)(2,1)}, bf16[2,128,256]{1,2,0:T(8,128)(2,1)S(1)}, u32[]{:S(2)}) copy-start(bf16[2,128,256]{1,2,0:T(8,128)(2,1)S(1)} %copy.452) | copy-start | bytes 393220
  55.5 1.4 copy-start.31
  55.5 1.7 copy-start.30
  55.8 1.7 copy-start.29
  56.2 1.6 copy-start.28
  56.5 4.3 %copy-start.8 = (bf16[2,128,256]{1,2,0:T(8,128)(2,1)}, bf16[2,128,256]{1,2,0:T(8,128)(2,1)S(1)}, u32[]{:S(2)}) copy-start(bf16[2,128,256]{1,2,0:T(8,128)(2,1)S(1)} %copy.465) | copy-start | bytes 393220
  56.5 1.7 copy-start.27
  62.2 1.2 copy-start.9
  90.7 1.6 copy-start.23
  90.8 3.0 %copy-start.22 = (f32[2,128,4,64]{1,3,2,0:T(8,128)S(1)}, f32[2,128,4,64]{1,3,2,0:T(8,128)}, u32[]{:S(2)}) copy-start(f32[2,128,4,64]{1,3,2,0:T(8,128)} %convolution_bitcast_fusion.3) | copy-start | bytes 786436
  92.3 2.9 %copy-start.21 = (f32[2,128,4,64]{1,3,2,0:T(8,128)S(1)}, f32[2,128,4,64]{1,3,2,0:T(8,128)}, u32[]{:S(2)}) copy-start(f32[2,128,4,64]{1,3,2,0:T(8,128)} %convolution_bitcast_fusion.4) | copy-start | bytes 786436
  92.5 4.1 %copy-start.20 = (f32[2,128,4,64]{1,3,2,0:T(8,128)S(1)}, f32[2,128,4,64]{1,3,2,0:T(8,128)}, u32[]{:S(2)}) copy-start(f32[2,128,4,64]{1,3,2,0:T(8,128)} %convolution_bitcast_fusion.5) | copy-start | bytes 786436
  94.0 4.1 %copy-start.19 = (f32[2,128,4,64]{1,3,2,0:T(8,128)S(1)}, f32[2,128,4,64]{1,3,2,0:T(8,128)}, u32[]{:S(2)}) copy-start(f32[2,128,4,64]{1,3,2,0:T(8,128)} %convolution_bitcast_fusion.6) | copy-start | bytes 786436
  95.4 4.1 %copy-start.18 = (f32[2,128,4,64]{1,3,2,0:T(8,128)S(1)}, f32[2,128,4,64]{1,3,2,0:T(8,128)}, u32[]{:S(2)}) copy-start(f32[2,128,4,64]{1,3,2,0:T(8,128)} %convolution_bitcast_fusion.7) | copy-start | bytes 786436
  96.9 4.1 %copy-start.17 = (f32[2,128,4,64]{1,3,2,0:T(8,128)S(1)}, f32[2,128,4,64]{1,3,2,0:T(8,128)}, u32[]{:S(2)}) copy-start(f32[2,128,4,64]{1,3,2,0:T(8,128)} %convolution_bitcast_fusion.8) | copy-start | bytes 786436
  109.1 1.0 copy-start.15
  109.1 8.2 %copy-start.14 = (f32[2,32768]{1,0:T(2,128)S(1)}, f32[2,32768]{1,0:T(2,128)}, u32[]{:S(2)}) copy-start(f32[2,32768]{1,0:T(2,128)} %get-tuple-element.18) | copy-start | bytes 786436
  109.1 11.6 %copy-start.13 = (f32[2,32768]{1,0:T(2,128)S(1)}, f32[2,32768]{1,0:T(2,128)}, u32[]{:S(2)}) copy-start(f32[2,32768]{1,0:T(2,128)} %get-tuple-element.17) | copy-start | bytes 786436
  109.8 16.5 %copy-start.12 = (f32[2,32768]{1,0:T(2,128)S(1)}, f32[2,32768]{1,0:T(2,128)}, u32[]{:S(2)}) copy-start(f32[2,32768]{1,0:T(2,128)} %get-tuple-element.16) | copy-start | bytes 786436
  110.0 20.4 %copy-start.11 = (f32[2,32768]{1,0:T(2,128)S(1)}, f32[2,32768]{1,0:T(2,128)}, u32[]{:S(2)}) copy-start(f32[2,32768]{1,0:T(2,128)} %get-tuple-element.15) | copy-start | bytes 786436
  110.3 24.7 %collective-permute-start.6 = (f32[2,2,128,256]{3,1,2,0:T(2,128)S(1)}, f32[2,2,128,256]{3,1,2,0:T(2,128)S(1)}, u32[]{:S(2)}, u32[]{:S(2)}) collective-permute-start(f32[2,2,128,256]{3,1,2,0:T(2,128)S(1)} %pad_maximum_fusion.1), channel_id=1, source_target_pairs={{4,0},{8,4},{12,8},{16,12},{20,16},{24,20},{28,24},{32,28},{36,32}... | collective-permute-start | bytes 1572872 | tf_op jit(solution)/shard_map/ppermute | solution.py:14
  117.3 16.1 %copy-start.10 = (f32[2,32768]{1,0:T(2,128)S(1)}, f32[2,32768]{1,0:T(2,128)}, u32[]{:S(2)}) copy-start(f32[2,32768]{1,0:T(2,128)} %get-tuple-element.14) | copy-start | bytes 786436
  118.4 23.7 %collective-permute-start.7 = (f32[2,2,128,256]{3,1,2,0:T(2,128)}, f32[2,2,128,256]{3,1,2,0:T(2,128)S(1)}, u32[]{:S(2)}, u32[]{:S(2)}) collective-permute-start(f32[2,2,128,256]{3,1,2,0:T(2,128)} %pad_maximum_fusion.2), channel_id=1, source_target_pairs={{0,4},{4,8},{8,12},{12,16},{16,20},{20,24},{24,28},{28,32},{32,36}... | collective-permute-start | bytes 1572872 | tf_op jit(solution)/shard_map/ppermute | solution.py:14
  120.7 13.8 %copy-start.5 = (bf16[2,128,256]{1,2,0:T(8,128)(2,1)S(1)}, bf16[2,128,256]{1,2,0:T(8,128)(2,1)}, u32[]{:S(2)}) copy-start(bf16[2,128,256]{1,2,0:T(8,128)(2,1)} %copy-done.4) | copy-start | bytes 393220
  120.7 13.8 %copy-start.16 = (f32[2,4,64,128]{3,2,1,0:T(8,128)S(1)}, f32[2,4,64,128]{3,2,1,0:T(8,128)}, u32[]{:S(2)}) copy-start(f32[2,4,64,128]{3,2,1,0:T(8,128)} %convolution_add_fusion.5) | copy-start | bytes 786436
  121.8 12.9 %copy-start.3 = (bf16[2,128,256]{1,2,0:T(8,128)(2,1)S(1)}, bf16[2,128,256]{1,2,0:T(8,128)(2,1)}, u32[]{:S(2)}) copy-start(bf16[2,128,256]{1,2,0:T(8,128)(2,1)} %copy-done.2) | copy-start | bytes 393220
  121.8 20.3 %collective-permute-start.8 = (f32[2,2,128,256]{3,1,2,0:T(2,128)}, f32[2,2,128,256]{3,1,2,0:T(2,128)S(1)}, u32[]{:S(2)}, u32[]{:S(2)}) collective-permute-start(f32[2,2,128,256]{3,1,2,0:T(2,128)} %pad_maximum_fusion.3), channel_id=1, source_target_pairs={{8,0},{12,4},{16,8},{20,12},{24,16},{28,20},{32,24},{36,28},{40,32... | collective-permute-start | bytes 1572872 | tf_op jit(solution)/shard_map/ppermute | solution.py:14
  127.3 13.8 %copy-start.1 = (bf16[2,128,256]{1,2,0:T(8,128)(2,1)S(1)}, bf16[2,128,256]{1,2,0:T(8,128)(2,1)}, u32[]{:S(2)}) copy-start(bf16[2,128,256]{1,2,0:T(8,128)(2,1)} %copy-done) | copy-start | bytes 393220
  127.3 16.3 %collective-permute-start.9 = (f32[2,2,128,256]{3,1,2,0:T(2,128)}, f32[2,2,128,256]{3,1,2,0:T(2,128)}, u32[]{:S(2)}, u32[]{:S(2)}) collective-permute-start(f32[2,2,128,256]{3,1,2,0:T(2,128)} %pad_maximum_fusion.4), channel_id=1, source_target_pairs={{0,8},{4,12},{8,16},{12,20},{16,24},{20,28},{24,32},{28,36},{32,40... | collective-permute-start | bytes 1572872 | tf_op jit(solution)/shard_map/ppermute | solution.py:14
  131.5 18.3 %collective-permute-start.10 = (f32[2,2,128,256]{3,1,2,0:T(2,128)}, f32[2,2,128,256]{3,1,2,0:T(2,128)}, u32[]{:S(2)}, u32[]{:S(2)}) collective-permute-start(f32[2,2,128,256]{3,1,2,0:T(2,128)} %pad_maximum_fusion.5), channel_id=1, source_target_pairs={{12,0},{16,4},{20,8},{24,12},{28,16},{32,20},{36,24},{40,28},{44,3... | collective-permute-start | bytes 1572872 | tf_op jit(solution)/shard_map/ppermute | solution.py:14
  133.4 8.1 %copy-start.7 = (bf16[2,128,256]{1,2,0:T(8,128)(2,1)S(1)}, bf16[2,128,256]{1,2,0:T(8,128)(2,1)}, u32[]{:S(2)}) copy-start(bf16[2,128,256]{1,2,0:T(8,128)(2,1)} %copy-done.6) | copy-start | bytes 393220
  134.7 34.6 %copy-start.24 = (f32[2,32768]{1,0:T(2,128)S(1)}, f32[2,32768]{1,0:T(2,128)}, u32[]{:S(2)}) copy-start(f32[2,32768]{1,0:T(2,128)} %get-tuple-element.13) | copy-start | bytes 786436
  134.9 7.0 %copy-start.25 = (bf16[2,4,64,128]{3,2,1,0:T(8,128)(2,1)S(1)}, bf16[2,4,64,128]{3,2,1,0:T(8,128)(2,1)}, u32[]{:S(2)}) copy-start(bf16[2,4,64,128]{3,2,1,0:T(8,128)(2,1)} %get-tuple-element.84) | copy-start | bytes 393220
  134.9 34.3 %collective-permute-start.11 = (f32[2,2,128,256]{3,1,2,0:T(2,128)}, f32[2,2,128,256]{3,1,2,0:T(2,128)}, u32[]{:S(2)}, u32[]{:S(2)}) collective-permute-start(f32[2,2,128,256]{3,1,2,0:T(2,128)} %pad_maximum_fusion.6), channel_id=1, source_target_pairs={{0,12},{4,16},{8,20},{12,24},{16,28},{20,32},{24,36},{28,40},{32,4... | collective-permute-start | bytes 1572872 | tf_op jit(solution)/shard_map/ppermute | solution.py:14
where the time goes:
time: 186 us; the launch traced here: 184 us
  local copies, waits for them, and re-layouts  50.4 us (27%)
  starting transfers between devices  47.7 us (26%)
  waiting for transfers between devices  43.7 us (23%)
  matrix products  20.3 us (11%)
  other arithmetic  10.9 us (6%)
  blocking collectives  9.33 us (5%)
    ppermute x12, starting transfers between devices, passed_along(): lax.ppermute(value, axis, [(source, source + steps) for source in range(l...  43.5 us
    ppermute x12, waiting for transfers between devices, passed_along(): lax.ppermute(value, axis, [(source, source + steps) for source in range(l...  36.2 us
    another operation x8, local copies, waits for them, and re-layouts, attend(): jnp.stack(key_list).reshape(slot_count, frame_count, token_count * width)  13.7 us
    another operation x8, local copies, waits for them, and re-layouts, attend(): jnp.stack(value_list).reshape(slot_count, frame_count, token_count * width)  13.5 us
    all_to_all x1, blocking collectives, in_one_piece(): lax.all_to_all(both, axis, split_axis=split_dim, concat_axis=concat_dim,...  9.33 us
    all_to_all x1, waiting for transfers between devices, in_one_piece(): lax.all_to_all(both, axis, split_axis=split_dim, concat_axis=concat_dim,...  7.45 us
    dot_general x7, matrix products, attend(): jnp.einsum('ahqk,aqhd->akhd', rounded, grad_four, preferred_element_type=...  7.05 us
    unnamed x75, local copies, waits for them, and re-layouts  6.5 us
  transfers between devices with their start and end apart: 13, of which 7 were waited for; matrix products, arithmetic and copies ran while one was open for 6% of the time, Pallas kernels for 0%

commit v1 on v0

v1 whole, which is shorter than its diff:
```python
import functools

import jax
import jax.numpy as jnp
from jax import lax
from jax.experimental import pallas as pl
from jax.experimental.pallas import tpu as pltpu
from jax.sharding import PartitionSpec as P

HEAD_DIM = 64
SLOTS = 6
KEYS = SLOTS + 1
HALO = 6
OWN = 8
WIN = OWN + 2 * HALO
TOK = 128
HEADS = 16
ZERO = OWN * KEYS
MESH = pl.DeviceIdType.MESH
SCALE = float(HEAD_DIM) ** -0.5
OFFSETS = sorted(
    [(dx, dy) for dx in range(4) for dy in range(4)],
    key=lambda o: -(min(o[0], 4 - o[0]) + min(o[1], 4 - o[1])),
)


def kernel(
    chain,
    q_hbm,
    k_hbm,
    v_hbm,
    g_hbm,
    part_hbm,
    att_ref,
    qg_ref,
    kg_ref,
    vg_ref,
    inb,
    stage,
    win,
    wint,
    own_qd,
    sc,
    pd,
    terms,
    ret_out,
    ret_in,
    acc,
    outs,
    ostage,
    part,
    table,
    in_sem,
    part_sem,
    send_sem,
    recv_sem,
    halo_send,
    halo_recv,
    ret_send,
    ret_recv,
    out_send,
    out_recv,
):
    fi = lax.axis_index("frames")
    y = lax.axis_index("heads")
    z = lax.div(fi, 8)
    x = lax.rem(lax.div(fi, 2), 4)
    c = lax.rem(fi, 2)
    pos = z * 2 + c
    head = y * 4 + x
    up = jnp.where(c == 0, fi + 1, fi + 7)
    down = jnp.where(c == 1, fi - 1, fi - 7)
    has_up = pos < chain - 1
    has_down = pos > 0
    stays = lax.div(x, 2) == c

    loads = [
        pltpu.make_async_copy(ref, inb.at[i], in_sem.at[i])
        for i, ref in enumerate((k_hbm, v_hbm, q_hbm, g_hbm))
    ]
    for copy in loads:
        copy.start()
    part_copy = pltpu.make_async_copy(
        part_hbm.at[pl.ds(pl.multiple_of(pos * OWN, OWN), OWN), :], part, part_sem
    )
    part_copy.start()

    barrier = pltpu.get_barrier_semaphore()
    for j in range(2):
        for cs in range(2):
            for dy in range(4):
                ys = lax.rem(y + dy, 4)
                xs = 2 * c + j
                if dy == 0:

                    @pl.when(jnp.logical_or(xs != x, cs != c))
                    def _():
                        pl.semaphore_signal(
                            barrier, inc=1, device_id=(z * 8 + xs * 2 + cs, ys), device_id_type=MESH
                        )
                else:
                    pl.semaphore_signal(
                        barrier, inc=1, device_id=(z * 8 + xs * 2 + cs, ys), device_id_type=MESH
                    )

    @pl.when(has_up)
    def _():
        pl.semaphore_signal(barrier, inc=1, device_id=(up, y), device_id_type=MESH)

    @pl.when(has_down)
    def _():
        pl.semaphore_signal(barrier, inc=1, device_id=(down, y), device_id_type=MESH)

    lane = lax.broadcasted_iota(jnp.int32, (2, 32, 128), 2)
    low = lane < HEAD_DIM

    def turned(value):
        return jnp.concatenate([value[..., HEAD_DIM:], value[..., :HEAD_DIM]], axis=-1)

    def pack(kind, first, second, scale):
        for p in range(HEADS // 2):
            one = inb[first, :, :, p * 128 : (p + 1) * 128]
            two = inb[second, :, :, p * 128 : (p + 1) * 128]
            if scale:
                one = one * jnp.bfloat16(SCALE)
            stage[kind, 2 * p] = jnp.where(low, one, turned(two))
            stage[kind, 2 * p + 1] = jnp.where(low, turned(one), two)

    loads[0].wait()
    loads[1].wait()
    pack(0, 0, 1, False)
    loads[2].wait()
    loads[3].wait()
    pack(1, 2, 3, True)

    pl.semaphore_wait(
        barrier,
        16
        - stays.astype(jnp.int32)
        + has_up.astype(jnp.int32)
        + has_down.astype(jnp.int32),
    )

    pair = lax.rem(x, 2) * 2 + c
    rows = pl.ds(pl.multiple_of(y * 32, 32), 32)
    sends = []
    for kind in range(2):
        for i, (dx, dy) in enumerate(OFFSETS):
            xd = lax.rem(x + dx, 4)
            yd = lax.rem(y + dy, 4)
            src = stage.at[kind, yd * 4 + xd]
            if kind == 0:
                dst = win.at[pl.ds(HALO + 2 * pair, 2), rows, :]
            else:
                dst = own_qd.at[pl.ds(2 * pair, 2), rows, :]
            remote = pltpu.make_async_remote_copy(
                src_ref=src,
                dst_ref=dst,
                send_sem=send_sem.at[kind, i],
                recv_sem=recv_sem.at[kind, pair],
                device_id=(z * 8 + xd * 2 + lax.div(x, 2), yd),
                device_id_type=MESH,
            )
            if dx == 0 and dy == 0:
                local = pltpu.make_async_copy(src, dst, recv_sem.at[kind, pair])

                @pl.when(stays)
                def _():
                    local.start()

                @pl.when(jnp.logical_not(stays))
                def _():
                    remote.start()

                sends.append((True, remote))
            else:
                remote.start()
                sends.append((False, remote))

    part_copy.wait()

    base = pos * OWN - HALO

    @pl.loop(0, OWN)
    def _(f):
        for w in range(WIN):
            at = jnp.int32(ZERO)
            for s in range(SLOTS):
                at = jnp.where(part[f, s] - base == w, f * KEYS + 1 + s, at)
            at = jnp.where(f + HALO == w, f * KEYS, at)
            table[f, w] = at

    terms[ZERO] = jnp.zeros((TOK, 128), jnp.float32)

    @pl.when(jnp.logical_not(has_up))
    def _():
        win[HALO + OWN :] = jnp.zeros((HALO, TOK, 128), jnp.bfloat16)
        ret_in[0] = jnp.zeros((HALO, TOK, 128), jnp.bfloat16)

    @pl.when(jnp.logical_not(has_down))
    def _():
        win[:HALO] = jnp.zeros((HALO, TOK, 128), jnp.bfloat16)
        ret_in[1] = jnp.zeros((HALO, TOK, 128), jnp.bfloat16)

    halo_up = []
    halo_down = []
    for k in range(4):
        here = win.at[HALO + 2 * k : HALO + 2 * k + 2]
        pltpu.make_async_copy(here, here, recv_sem.at[0, k]).wait()
        if k >= 1:
            copy = pltpu.make_async_remote_copy(
                src_ref=here,
                dst_ref=win.at[2 * k - 2 : 2 * k],
                send_sem=halo_send.at[0, k - 1],
                recv_sem=halo_recv.at[0, k - 1],
                device_id=(up, y),
                device_id_type=MESH,
            )
            pl.when(has_up)(copy.start)
            halo_up.append(copy)
        if k <= 2:
            copy = pltpu.make_async_remote_copy(
                src_ref=here,
                dst_ref=win.at[HALO + OWN + 2 * k : HALO + OWN + 2 * k + 2],
                send_sem=halo_send.at[1, k],
                recv_sem=halo_recv.at[1, k],
                device_id=(down, y),
                device_id_type=MESH,
            )
            pl.when(has_down)(copy.start)
            halo_down.append(copy)

    def flip(w):
        wint[w] = win[w].T

    for f in range(OWN):
        flip(HALO + f)

    for copy in halo_up:
        pl.when(has_down)(copy.wait_recv)
    for copy in halo_down:
        pl.when(has_up)(copy.wait_recv)
    for w in range(HALO):
        flip(w)
        flip(HALO + OWN + w)
    for k in range(4):
        here = own_qd.at[2 * k : 2 * k + 2]
        pltpu.make_async_copy(here, here, recv_sem.at[1, k]).wait()

    half = lax.broadcasted_iota(jnp.int32, (TOK, 128), 1) < HEAD_DIM

    def one_frame(f):
        mixed = own_qd[f]
        none = jnp.zeros_like(mixed)
        qd = jnp.concatenate([jnp.where(half, none, mixed), jnp.where(half, mixed, none)], axis=0)
        at = [f + HALO]
        bias = [None]
        for s in range(SLOTS):
            partner = part[f, s]
            near = jnp.minimum(jnp.maximum(partner - base, 0), WIN - 1)
            at.append(jnp.where(partner >= 0, near, f + HALO))
            bias.append(jnp.where(partner >= 0, jnp.float32(0.0), jnp.float32(-jnp.inf)))
        peak = None
        for s in range(KEYS):
            both = lax.dot_general(
                win[at[s]], qd, (((1,), (1,)), ((), ())), preferred_element_type=jnp.float32
            )
            score = both[:, 128:]
            if bias[s] is not None:
                score = score + bias[s]
            sc[s, :, :128] = both[:, :128]
            sc[s, :, 128:] = score
            top = jnp.max(score.reshape(16, 8, 128), axis=0)
            peak = top if peak is None else jnp.maximum(peak, top)
        peak = jnp.max(peak, axis=0, keepdims=True)
        total = jnp.zeros((8, 128), jnp.float32)
        dsum = jnp.zeros((8, 128), jnp.float32)
        for s in range(KEYS):
            e = jnp.exp(sc[s, :, 128:] - peak)
            sc[s, :, 128:] = e
            total = total + jnp.sum(e.reshape(16, 8, 128), axis=0)
            dsum = dsum + jnp.sum((e * sc[s, :, :128]).reshape(16, 8, 128), axis=0)
        inv = 1.0 / jnp.sum(total, axis=0, keepdims=True)
        delta = jnp.sum(dsum, axis=0, keepdims=True) * inv
        for s in range(KEYS):
            w = sc[s, :, 128:] * inv
            pd[s * TOK : (s + 1) * TOK, :128] = w.astype(jnp.bfloat16)
            pd[s * TOK : (s + 1) * TOK, 128:] = (w * (sc[s, :, :128] - delta)).astype(jnp.bfloat16)
        prod = jnp.dot(pd[...], qd, preferred_element_type=jnp.float32)
        for s in range(KEYS):
            terms[f * KEYS + s] = prod[s * TOK : (s + 1) * TOK]
        turned_kv = jnp.concatenate([wint[at[s]] for s in range(KEYS)], axis=1)
        res = jnp.dot(turned_kv, pd[...], preferred_element_type=jnp.float32)
        outcome = jnp.concatenate([res[:HEAD_DIM, 128:] * SCALE, res[HEAD_DIM:, :128]], axis=0)
        outs[0, f] = outcome.T.astype(jnp.bfloat16)

    out_copies = []

    def give_back(kind, k):
        xs = 2 * c + k // 2
        cs = k % 2
        for dy in range(4):
            ys = lax.rem(y + dy, 4)
            src = outs.at[kind, 2 * k : 2 * k + 2, pl.ds(pl.multiple_of(ys * 32, 32), 32), :]
            dst = ostage.at[kind, head]
            remote = pltpu.make_async_remote_copy(
                src_ref=src,
                dst_ref=dst,
                send_sem=out_send.at[kind, k, dy],
                recv_sem=out_recv.at[kind],
                device_id=(z * 8 + xs * 2 + cs, ys),
                device_id_type=MESH,
            )
            if dy == 0:
                mine = jnp.logical_and(xs == x, cs == c)
                local = pltpu.make_async_copy(src, dst, out_recv.at[kind])
                pl.when(mine)(local.start)
                pl.when(jnp.logical_not(mine))(remote.start)
                out_copies.append((mine, remote))
            else:
                remote.start()
                out_copies.append((None, remote))

    @pl.loop(0, OWN)
    def _(f):
        one_frame(f)

    for k in range(4):
        give_back(0, k)

    def gathered(w):
        total = None
        for f in range(max(0, w - 2 * HALO), min(OWN, w + 1)):
            term = terms[table[f, w]]
            total = term if total is None else total + term
        return total

    for w in range(HALO):
        ret_out[0, w] = gathered(w).astype(jnp.bfloat16)
    back_down = pltpu.make_async_remote_copy(
        src_ref=ret_out.at[0],
        dst_ref=ret_in.at[0],
        send_sem=ret_send.at[0],
        recv_sem=ret_recv.at[0],
        device_id=(down, y),
        device_id_type=MESH,
    )
    pl.when(has_down)(back_down.start)
    for w in range(HALO):
        ret_out[1, w] = gathered(HALO + OWN + w).astype(jnp.bfloat16)
    back_up = pltpu.make_async_remote_copy(
        src_ref=ret_out.at[1],
        dst_ref=ret_in.at[1],
        send_sem=ret_send.at[1],
        recv_sem=ret_recv.at[1],
        device_id=(up, y),
        device_id_type=MESH,
    )
    pl.when(has_up)(back_up.start)
    for f in range(OWN):
        acc[f] = gathered(HALO + f)
    pl.when(has_up)(back_down.wait_recv)
    pl.when(has_down)(back_up.wait_recv)
    for k in range(4):
        for f in (2 * k, 2 * k + 1):
            total = acc[f]
            if f >= 2:
                total = total + ret_in[0, f - 2].astype(jnp.float32)
            if f < HALO:
                total = total + ret_in[1, f].astype(jnp.float32)
            outs[1, f] = total.astype(jnp.bfloat16)
        give_back(1, k)

    def unpack(kind, one_ref, two_ref):
        pltpu.make_async_copy(ostage.at[kind], ostage.at[kind], out_recv.at[kind]).wait()
        for p in range(HEADS // 2):
            even = ostage[kind, 2 * p]
            odd = ostage[kind, 2 * p + 1]
            one_ref[:, :, p * 128 : (p + 1) * 128] = jnp.where(low, even, turned(odd))
            two_ref[:, :, p * 128 : (p + 1) * 128] = jnp.where(low, turned(even), odd)

    unpack(0, qg_ref, att_ref)
    unpack(1, kg_ref, vg_ref)

    for local_too, remote in sends:
        if local_too:
            pl.when(jnp.logical_not(stays))(remote.wait_send)
        else:
            remote.wait_send()
    for copy in halo_up:
        pl.when(has_up)(copy.wait_send)
    for copy in halo_down:
        pl.when(has_down)(copy.wait_send)
    pl.when(has_down)(back_down.wait_send)
    pl.when(has_up)(back_up.wait_send)
    for mine, remote in out_copies:
        if mine is None:
            remote.wait_send()
        else:
            pl.when(jnp.logical_not(mine))(remote.wait_send)


def per_device(query, keyed, valued, grad_out, partners):
    chain = lax.axis_size("frames") // 4
    shape = jax.ShapeDtypeStruct(query.shape, jnp.bfloat16)
    dma = pltpu.SemaphoreType.DMA
    return pl.pallas_call(
        functools.partial(kernel, chain),
        out_shape=(shape,) * 4,
        in_specs=[pl.BlockSpec(memory_space=pl.ANY)] * 5,
        out_specs=(pl.BlockSpec(memory_space=pltpu.VMEM),) * 4,
        scratch_shapes=[
            pltpu.VMEM((4, 2, 32, 1024), jnp.bfloat16),
            pltpu.VMEM((2, HEADS, 2, 32, 128), jnp.bfloat16),
            pltpu.VMEM((WIN, TOK, 128), jnp.bfloat16),
            pltpu.VMEM((WIN, 128, TOK), jnp.bfloat16),
            pltpu.VMEM((OWN, TOK, 128), jnp.bfloat16),
            pltpu.VMEM((KEYS, TOK, 256), jnp.float32),
            pltpu.VMEM((KEYS * TOK, 256), jnp.bfloat16),
            pltpu.VMEM((ZERO + 1, TOK, 128), jnp.float32),
            pltpu.VMEM((2, HALO, TOK, 128), jnp.bfloat16),
            pltpu.VMEM((2, HALO, TOK, 128), jnp.bfloat16),
            pltpu.VMEM((OWN, TOK, 128), jnp.float32),
            pltpu.VMEM((2, OWN, TOK, 128), jnp.bfloat16),
            pltpu.VMEM((2, HEADS, 2, 32, 128), jnp.bfloat16),
            pltpu.SMEM((OWN, SLOTS), jnp.int32),
            pltpu.SMEM((OWN, WIN), jnp.int32),
            dma((4,)),
            dma(()),
            dma((2, 16)),
            dma((2, 4)),
            dma((2, 3)),
            dma((2, 3)),
            dma((2,)),
            dma((2,)),
            dma((2, 4, 4)),
            dma((2,)),
        ],
        compiler_params=pltpu.CompilerParams(
            collective_id=0, has_side_effects=True, vmem_limit_bytes=48 * 2**20
        ),
    )(query, keyed, valued, grad_out, partners)


def solution(mesh):
    spec = P("frames", "heads", None)
    return jax.shard_map(
        per_device,
        mesh=mesh,
        in_specs=(spec, spec, spec, spec, P()),
        out_specs=(spec,) * 4,
        check_vma=False,
    )
```

time: 186 us -> 45 us (0.24)
  the two profiles are of different devices: /device:TPU:135 before, /device:TPU:385 now
where the time goes in v1:
time: 45 us; the launch traced here: 44.8 us
  Pallas kernels  37.9 us (84%)
  local copies, waits for them, and re-layouts  6.24 us (14%)
  between operations  0.66 us (1%)
    pallas_call x1, Pallas kernels, per_device(): pl.pallas_call(functools.partial(kernel, chain), out_shape=(shape,) * 4,...  37.9 us
    unnamed x13, local copies, waits for them, and re-layouts  6.24 us

profile of v1, /device:TPU:385, one launch (start us, length us, event | category | flops | bytes accessed | tf_op | source)
XLA Modules:
  0.0 44.8 jit_solution(14044219725638754121)
XLA Ops:
  0.6 0.0 copy-start
  0.6 0.9 %copy.9.part_hbm = s32[256,6]{1,0:T(8,128)S(1)} copy(s32[256,6]{0,1:T(8,128)} %param.9) | data formatting | bytes 12288 | tf_op args[4]
  1.5 0.0 copy-done
  1.6 0.0 copy-start.1
  1.6 0.9 %copy-done.1 = bf16[2,32,1024]{2,1,0:T(8,128)(2,1)S(1)} copy-done((bf16[2,32,1024]{2,1,0:T(8,128)(2,1)S(1)}, bf16[2,32,1024]{2,1,0:T(8,128)(2,1)}, u32[]{:S(2)}) %copy-start.1) | copy-done | bytes 131096
  2.5 0.0 copy-start.2
  2.5 0.9 %copy-done.2 = bf16[2,32,1024]{2,1,0:T(8,128)(2,1)S(1)} copy-done((bf16[2,32,1024]{2,1,0:T(8,128)(2,1)S(1)}, bf16[2,32,1024]{2,1,0:T(8,128)(2,1)}, u32[]{:S(2)}) %copy-start.2) | copy-done | bytes 131096
  3.4 0.0 copy-start.3
  3.4 0.9 %copy-done.3 = bf16[2,32,1024]{2,1,0:T(8,128)(2,1)S(1)} copy-done((bf16[2,32,1024]{2,1,0:T(8,128)(2,1)S(1)}, bf16[2,32,1024]{2,1,0:T(8,128)(2,1)}, u32[]{:S(2)}) %copy-start.3) | copy-done | bytes 131096
  4.3 37.9 %shard_map.84 = (bf16[2,32,1024]{2,1,0:T(8,128)(2,1)S(1)}, bf16[2,32,1024]{2,1,0:T(8,128)(2,1)S(1)}, bf16[2,32,1024]{2,1,0:T(8,128)(2,1)S(1)}, bf16[2,32,1024]{2,1,0:T(8,128)(2,1)S(1)}) custom-call(bf16[2,32,1024]{2,1,0:T(8,128)(2,1)S(1)} %copy-done, bf16[2,32,1024]{2,1,0:T(8,128)(2,1)S(1)} %copy-done.1, bf16[2,32,1024]{2,1,0:T(8,128)(2,1)S(1)} %copy-done.2, ...), custom_call_target="tpu_custom_call" | custom-call | tf_op jit(solution)/shard_map/pallas_call | solution.py:407
  42.2 0.7 %copy.14 = bf16[2,32,1024]{2,1,0:T(8,128)(2,1)} copy(bf16[2,32,1024]{2,1,0:T(8,128)(2,1)S(1)} %get-tuple-element.8) | data formatting | bytes 262144
  42.9 0.7 %copy.15 = bf16[2,32,1024]{2,1,0:T(8,128)(2,1)} copy(bf16[2,32,1024]{2,1,0:T(8,128)(2,1)S(1)} %get-tuple-element.9) | data formatting | bytes 262144
  43.5 0.7 %copy.16 = bf16[2,32,1024]{2,1,0:T(8,128)(2,1)} copy(bf16[2,32,1024]{2,1,0:T(8,128)(2,1)S(1)} %get-tuple-element.10) | data formatting | bytes 262144
  44.2 0.7 %copy.17 = bf16[2,32,1024]{2,1,0:T(8,128)(2,1)} copy(bf16[2,32,1024]{2,1,0:T(8,128)(2,1)S(1)} %get-tuple-element.11) | data formatting | bytes 262144
Async XLA Ops:
  0.6 0.9 %copy-start = (bf16[2,32,1024]{2,1,0:T(8,128)(2,1)S(1)}, bf16[2,32,1024]{2,1,0:T(8,128)(2,1)}, u32[]{:S(2)}) copy-start(bf16[2,32,1024]{2,1,0:T(8,128)(2,1)} %q_hbm.1) | copy-start | bytes 393220
  1.6 0.9 %copy-start.1 = (bf16[2,32,1024]{2,1,0:T(8,128)(2,1)S(1)}, bf16[2,32,1024]{2,1,0:T(8,128)(2,1)}, u32[]{:S(2)}) copy-start(bf16[2,32,1024]{2,1,0:T(8,128)(2,1)} %k_hbm.1) | copy-start | bytes 393220
  2.5 0.9 %copy-start.2 = (bf16[2,32,1024]{2,1,0:T(8,128)(2,1)S(1)}, bf16[2,32,1024]{2,1,0:T(8,128)(2,1)}, u32[]{:S(2)}) copy-start(bf16[2,32,1024]{2,1,0:T(8,128)(2,1)} %v_hbm.1) | copy-start | bytes 393220
  3.4 0.9 %copy-start.3 = (bf16[2,32,1024]{2,1,0:T(8,128)(2,1)S(1)}, bf16[2,32,1024]{2,1,0:T(8,128)(2,1)}, u32[]{:S(2)}) copy-start(bf16[2,32,1024]{2,1,0:T(8,128)(2,1)} %g_hbm.1) | copy-start | bytes 393220

commit v2 on v1

v2 whole, which is shorter than its diff:
```python
import functools

import jax
import jax.numpy as jnp
from jax import lax
from jax.experimental import pallas as pl
from jax.experimental.pallas import tpu as pltpu
from jax.sharding import PartitionSpec as P

HEAD_DIM = 64
SLOTS = 6
KEYS = SLOTS + 1
HALO = 6
OWN = 8
WIN = OWN + 2 * HALO
TOK = 128
HEADS = 16
ZERO = OWN * KEYS
MESH = pl.DeviceIdType.MESH
SCALE = float(HEAD_DIM) ** -0.5
OFFSETS = sorted(
    [(dx, dy) for dx in range(4) for dy in range(4)],
    key=lambda o: -(min(o[0], 4 - o[0]) + min(o[1], 4 - o[1])),
)


def turned(value):
    return jnp.concatenate([value[..., HEAD_DIM:], value[..., :HEAD_DIM]], axis=-1)


def unpack_kernel(staged, att_hbm, qg_hbm, kg_hbm, vg_hbm, taken, whole, in_sem, sem):
    low = lax.broadcasted_iota(jnp.int32, (2, 32, 128), 2) < HEAD_DIM
    outs = (qg_hbm, att_hbm, kg_hbm, vg_hbm)
    loads = {}
    for kind in (0, 2, 1):
        for h in range(2):
            at = (kind, slice(h * 8, (h + 1) * 8))
            loads[kind, h] = pltpu.make_async_copy(staged.at[at], taken.at[at], in_sem.at[kind, h])
            loads[kind, h].start()
    copies = []
    for kind in range(2):
        for p in range(HEADS // 2):
            if p % 4 == 0:
                loads[kind, p // 4].wait()
                if kind == 1:
                    loads[2, p // 4].wait()
            at = slice(p * 128, (p + 1) * 128)
            even = taken[kind, 2 * p]
            odd = taken[kind, 2 * p + 1]
            if kind == 1:
                even = even + taken[2, 2 * p]
                odd = odd + taken[2, 2 * p + 1]
            whole[2 * kind, :, :, at] = jnp.where(low, even, turned(odd))
            whole[2 * kind + 1, :, :, at] = jnp.where(low, turned(even), odd)
        for i in (2 * kind, 2 * kind + 1):
            copies.append(pltpu.make_async_copy(whole.at[i], outs[i], sem.at[i]))
            copies[-1].start()
    for copy in copies:
        copy.wait()


def unpacked(staged, shape):
    return pl.pallas_call(
        unpack_kernel,
        out_shape=(jax.ShapeDtypeStruct(shape, jnp.bfloat16),) * 4,
        in_specs=[pl.BlockSpec(memory_space=pltpu.HBM)],
        out_specs=(pl.BlockSpec(memory_space=pltpu.HBM),) * 4,
        scratch_shapes=[
            pltpu.VMEM(staged.shape, jnp.bfloat16),
            pltpu.VMEM((4,) + shape, jnp.bfloat16),
            pltpu.SemaphoreType.DMA((3, 2)),
            pltpu.SemaphoreType.DMA((4,)),
        ],
    )(staged)


def kernel(
    depth,
    q_hbm,
    k_hbm,
    v_hbm,
    g_hbm,
    part_hbm,
    ostage,
    inb,
    stage,
    win,
    wint,
    own_qd,
    sc,
    pd,
    terms,
    cross_out,
    die_out,
    die_in,
    outs,
    blank,
    part,
    table,
    in_sem,
    part_sem,
    send_sem,
    recv_sem,
    cross_send,
    cross_recv,
    die_send,
    die_recv,
    ret_send,
    ret_recv,
    out_send,
    cross_out_send,
    out_recv,
):
    fi = lax.axis_index("frames")
    y = lax.axis_index("heads")
    z = lax.div(fi, 8)
    x = lax.rem(lax.div(fi, 2), 4)
    c = lax.rem(fi, 2)
    pos = z * 2 + c
    head = y * 4 + x
    home = lax.div(x, 2)
    pair = lax.rem(x, 2) * 2 + c
    stays = home == c
    partner = fi + 1 - 2 * c
    ahead = jnp.logical_and(jnp.logical_and(home == 1, pair >= 1), z < depth - 1)
    behind = jnp.logical_and(jnp.logical_and(home == 0, pair <= 2), z > 0)
    crosses = jnp.logical_or(ahead, behind)
    has_cross = jnp.logical_or(jnp.logical_and(c == 1, z < depth - 1), jnp.logical_and(c == 0, z > 0))

    loads = [
        pltpu.make_async_copy(ref, inb.at[i], in_sem.at[i])
        for i, ref in enumerate((k_hbm, v_hbm, q_hbm, g_hbm))
    ]
    for copy in loads:
        copy.start()
    part_copy = pltpu.make_async_copy(part_hbm, part, part_sem)
    part_copy.start()

    barrier = pltpu.get_barrier_semaphore()

    def greet(frame_at, head_at):
        pl.semaphore_signal(barrier, inc=1, device_id=(frame_at, head_at), device_id_type=MESH)

    other = z + 2 * c - 1
    for j in range(2):
        for cs in range(2):
            xs = 2 * c + j
            xo = 2 * (1 - c) + j
            for dy in range(4):
                ys = lax.rem(y + dy, 4)
                if dy == 0:

                    @pl.when(jnp.logical_or(xs != x, cs != c))
                    def _():
                        greet(z * 8 + xs * 2 + cs, ys)
                else:
                    greet(z * 8 + xs * 2 + cs, ys)
            if (j, cs) == (0, 0):
                wanted = jnp.logical_and(has_cross, c == 1)
            elif (j, cs) == (1, 1):
                wanted = jnp.logical_and(has_cross, c == 0)
            else:
                wanted = has_cross

            @pl.when(wanted)
            def _():
                for dy in range(4):
                    greet(other * 8 + xo * 2 + cs, lax.rem(y + dy, 4))

    greet(partner, y)

    low = lax.broadcasted_iota(jnp.int32, (2, 32, 128), 2) < HEAD_DIM

    def pack(kind, first, second, scale):
        for p in range(HEADS // 2):
            one = inb[first, :, :, p * 128 : (p + 1) * 128]
            two = inb[second, :, :, p * 128 : (p + 1) * 128]
            if scale:
                one = one * jnp.bfloat16(SCALE)
            stage[kind, 2 * p] = jnp.where(low, one, turned(two))
            stage[kind, 2 * p + 1] = jnp.where(low, turned(one), two)

    loads[0].wait()
    loads[1].wait()
    pack(0, 0, 1, False)
    loads[2].wait()
    loads[3].wait()
    pack(1, 2, 3, True)

    pl.semaphore_wait(
        barrier, 17 - stays.astype(jnp.int32) + 16 * crosses.astype(jnp.int32)
    )

    rows = pl.ds(pl.multiple_of(y * 32, 32), 32)

    def to_slab(kind, i, act):
        dx, dy = OFFSETS[i]
        xd = lax.rem(x + dx, 4)
        yd = lax.rem(y + dy, 4)
        src = stage.at[kind, yd * 4 + xd]
        if kind == 0:
            dst = win.at[pl.ds(HALO + 2 * pair, 2), rows, :]
        else:
            dst = own_qd.at[pl.ds(2 * pair, 2), rows, :]
        remote = pltpu.make_async_remote_copy(
            src_ref=src,
            dst_ref=dst,
            send_sem=send_sem.at[kind, i],
            recv_sem=recv_sem.at[kind, pair],
            device_id=(z * 8 + xd * 2 + home, yd),
            device_id_type=MESH,
        )
        if dx == 0 and dy == 0:
            if act == "start":
                local = pltpu.make_async_copy(src, dst, recv_sem.at[kind, pair])
                pl.when(stays)(local.start)
                pl.when(jnp.logical_not(stays))(remote.start)
            else:
                pl.when(jnp.logical_not(stays))(remote.wait_send)
        elif act == "start":
            remote.start()
        else:
            remote.wait_send()

    def to_next_slab(i, act):
        dx, dy = OFFSETS[i]
        xd = lax.rem(x + dx, 4)
        yd = lax.rem(y + dy, 4)
        land = jnp.where(home == 1, 2 * pair - 2, HALO + OWN + 2 * pair)
        remote = pltpu.make_async_remote_copy(
            src_ref=stage.at[0, yd * 4 + xd],
            dst_ref=win.at[pl.ds(land, 2), rows, :],
            send_sem=cross_send.at[i],
            recv_sem=cross_recv,
            device_id=((z + 2 * home - 1) * 8 + xd * 2 + 1 - home, yd),
            device_id_type=MESH,
        )
        if act == "start":
            remote.start()
        else:
            remote.wait_send()

    for i in range(16):
        to_slab(0, i, "start")

    @pl.when(crosses)
    def _():
        for i in range(16):
            to_next_slab(i, "start")

    for i in range(16):
        to_slab(1, i, "start")

    part_copy.wait()

    base = pos * OWN - HALO

    def turned_frame(i):
        return jnp.where(c == 0, i, OWN - 1 - i)

    @pl.loop(0, OWN)
    def _(i):
        f = turned_frame(i)
        at_frame = pos * OWN + f
        for w in range(WIN):
            target = base + jnp.where(c == 0, w, WIN - 1 - w)
            at = jnp.int32(ZERO)
            for s in range(SLOTS):
                at = jnp.where(part[s, at_frame] == target, i * KEYS + 1 + s, at)
            table[i, w] = jnp.where(i + HALO == w, i * KEYS, at)

    terms[ZERO] = jnp.zeros((TOK, 128), jnp.float32)
    near = jnp.where(c == 0, HALO + OWN, 0)
    far = jnp.where(c == 0, 0, HALO + OWN)

    blank_copy = pltpu.make_async_copy(blank, ostage.at[2], out_recv.at[2])

    @pl.when(jnp.logical_not(crosses))
    def _():
        blank[...] = jnp.zeros_like(blank)
        blank_copy.start()

    @pl.when(jnp.logical_not(has_cross))
    def _():
        win[pl.ds(far, HALO)] = jnp.zeros((HALO, TOK, 128), jnp.bfloat16)

    def own_pair(k):
        return win.at[pl.ds(HALO + 2 * k, 2)]

    def byte_wait(ref, sem):
        pltpu.make_async_copy(ref, ref, sem).wait()

    def flip(w):
        wint[w] = win[w].T

    die_copies = []
    for j in range(3):
        k = j + 1 - c
        byte_wait(own_pair(k), recv_sem.at[0, k])
        copy = pltpu.make_async_remote_copy(
            src_ref=own_pair(k),
            dst_ref=win.at[pl.ds((HALO + OWN) * c + 2 * j, 2)],
            send_sem=die_send.at[j],
            recv_sem=die_recv.at[j],
            device_id=(partner, y),
            device_id_type=MESH,
        )
        copy.start()
        die_copies.append(copy)
    byte_wait(own_pair(3 * c), recv_sem.at[0, 3 * c])
    for f in range(OWN):
        flip(HALO + f)
    for copy in die_copies:
        copy.wait_recv()
    for w in range(HALO):
        flip(near + w)

    @pl.when(has_cross)
    def _():
        byte_wait(win.at[pl.ds(far, HALO)], cross_recv)

    for w in range(HALO):
        flip(far + w)
    for k in range(4):
        byte_wait(own_qd.at[2 * k : 2 * k + 2], recv_sem.at[1, k])

    half = lax.broadcasted_iota(jnp.int32, (TOK, 128), 1) < HEAD_DIM

    def one_frame(i):
        u = i % 2
        f = turned_frame(i)
        mixed = own_qd[f]
        none = jnp.zeros_like(mixed)
        qd = jnp.concatenate([jnp.where(half, none, mixed), jnp.where(half, mixed, none)], axis=0)
        at = [f + HALO]
        bias = [None]
        for s in range(SLOTS):
            listed = part[s, pos * OWN + f]
            close = jnp.minimum(jnp.maximum(listed - base, 0), WIN - 1)
            at.append(jnp.where(listed >= 0, close, f + HALO))
            bias.append(jnp.where(listed >= 0, jnp.float32(0.0), jnp.float32(-jnp.inf)))
        peak = None
        for s in range(KEYS):
            both = lax.dot_general(
                win[at[s]], qd, (((1,), (1,)), ((), ())), preferred_element_type=jnp.float32
            )
            score = both[:, 128:]
            if bias[s] is not None:
                score = score + bias[s]
            sc[u, s, :, :128] = both[:, :128]
            sc[u, s, :, 128:] = score
            top = jnp.max(score.reshape(16, 8, 128), axis=0)
            peak = top if peak is None else jnp.maximum(peak, top)
        peak = jnp.max(peak, axis=0, keepdims=True)
        total = jnp.zeros((8, 128), jnp.float32)
        dsum = jnp.zeros((8, 128), jnp.float32)
        for s in range(KEYS):
            e = jnp.exp(sc[u, s, :, 128:] - peak)
            sc[u, s, :, 128:] = e
            total = total + jnp.sum(e.reshape(16, 8, 128), axis=0)
            dsum = dsum + jnp.sum((e * sc[u, s, :, :128]).reshape(16, 8, 128), axis=0)
        inv = 1.0 / jnp.sum(total, axis=0, keepdims=True)
        delta = jnp.sum(dsum, axis=0, keepdims=True) * inv
        for s in range(KEYS):
            w = sc[u, s, :, 128:] * inv
            rows_at = slice(s * TOK, (s + 1) * TOK)
            pd[u, rows_at, :128] = w.astype(jnp.bfloat16)
            pd[u, rows_at, 128:] = (w * (sc[u, s, :, :128] - delta)).astype(jnp.bfloat16)
        prod = jnp.dot(pd[u], qd, preferred_element_type=jnp.float32)
        for s in range(KEYS):
            terms[i * KEYS + s] = prod[s * TOK : (s + 1) * TOK]
        turned_kv = jnp.concatenate([wint[at[s]] for s in range(KEYS)], axis=1)
        res = jnp.dot(turned_kv, pd[u], preferred_element_type=jnp.float32)
        outcome = jnp.concatenate([res[:HEAD_DIM, 128:] * SCALE, res[HEAD_DIM:, :128]], axis=0)
        outs[0, f] = outcome.T.astype(jnp.bfloat16)

    def gathered(w):
        total = None
        for i in range(max(0, w - 2 * HALO), min(OWN, w + 1)):
            term = terms[table[i, w]]
            total = term if total is None else total + term
        return total

    def pair_of(j):
        return jnp.where(c == 0, j, 3 - j)

    def give_back(kind, j, act):
        k = pair_of(j)
        xs = 2 * c + lax.div(k, 2)
        cs = lax.rem(k, 2)
        for dy in range(4):
            ys = lax.rem(y + (2, 1, 3, 0)[dy], 4)
            src = outs.at[kind, pl.ds(2 * k, 2), pl.ds(pl.multiple_of(ys * 32, 32), 32), :]
            dst = ostage.at[kind, head]
            remote = pltpu.make_async_remote_copy(
                src_ref=src,
                dst_ref=dst,
                send_sem=out_send.at[kind, j, dy],
                recv_sem=out_recv.at[kind],
                device_id=(z * 8 + xs * 2 + cs, ys),
                device_id_type=MESH,
            )
            if dy == 3:
                mine = jnp.logical_and(xs == x, cs == c)
                if act == "start":
                    local = pltpu.make_async_copy(src, dst, out_recv.at[kind])
                    pl.when(mine)(local.start)
                    pl.when(jnp.logical_not(mine))(remote.start)
                else:
                    pl.when(jnp.logical_not(mine))(remote.wait_send)
            elif act == "start":
                remote.start()
            else:
                remote.wait_send()

    def give_across(j, act):
        k = jnp.where(c == 0, 1 + j, 2 - j)
        xs = 2 * (1 - c) + lax.div(k, 2)
        cs = lax.rem(k, 2)
        for dy in range(4):
            ys = lax.rem(y + (2, 1, 3, 0)[dy], 4)
            remote = pltpu.make_async_remote_copy(
                src_ref=cross_out.at[j, :, pl.ds(pl.multiple_of(ys * 32, 32), 32), :],
                dst_ref=ostage.at[2, head],
                send_sem=cross_out_send.at[j, dy],
                recv_sem=out_recv.at[2],
                device_id=(other * 8 + xs * 2 + cs, ys),
                device_id_type=MESH,
            )
            if act == "start":
                remote.start()
            else:
                remote.wait_send()

    for j in range(4):
        one_frame(2 * j)
        one_frame(2 * j + 1)
        give_back(0, j, "start")
        if j < 3:

            @pl.when(has_cross)
            def _():
                for half_at in range(2):
                    place = jnp.where(c == 0, half_at, 1 - half_at)
                    cross_out[j, place] = gathered(2 * j + half_at).astype(jnp.bfloat16)
                give_across(j, "start")

    ret_copies = []
    for j in range(3):
        for q in (2 * j, 2 * j + 1):
            die_out[q] = gathered(HALO + OWN + q).astype(jnp.bfloat16)
        copy = pltpu.make_async_remote_copy(
            src_ref=die_out.at[2 * j : 2 * j + 2],
            dst_ref=die_in.at[2 * j : 2 * j + 2],
            send_sem=ret_send.at[j],
            recv_sem=ret_recv.at[j],
            device_id=(partner, y),
            device_id_type=MESH,
        )
        copy.start()
        ret_copies.append(copy)
    for j in (0, 3, 2, 1):
        sums = [gathered(HALO + i) for i in (2 * j, 2 * j + 1)]
        if j > 0:
            ret_copies[3 - j].wait_recv()
        for n, i in enumerate((2 * j, 2 * j + 1)):
            total = sums[n]
            if j > 0:
                total = total + die_in[OWN - 1 - i].astype(jnp.float32)
            outs[1, turned_frame(i)] = total.astype(jnp.bfloat16)
        give_back(1, j, "start")

    for i in range(16):
        to_slab(0, i, "wait")
        to_slab(1, i, "wait")

    @pl.when(crosses)
    def _():
        for i in range(16):
            to_next_slab(i, "wait")

    for copy in die_copies + ret_copies:
        copy.wait_send()
    for j in range(4):
        give_back(0, j, "wait")
        give_back(1, j, "wait")

    @pl.when(has_cross)
    def _():
        for j in range(3):
            give_across(j, "wait")

    for kind in range(3):
        byte_wait(ostage.at[kind], out_recv.at[kind])


def per_device(query, keyed, valued, grad_out, partners):
    depth = lax.axis_size("frames") // 8
    dma = pltpu.SemaphoreType.DMA
    staged = pl.pallas_call(
        functools.partial(kernel, depth),
        out_shape=jax.ShapeDtypeStruct((3, HEADS, 2, 32, 128), jnp.bfloat16),
        in_specs=[pl.BlockSpec(memory_space=pltpu.HBM)] * 5,
        out_specs=pl.BlockSpec(memory_space=pltpu.HBM),
        scratch_shapes=[
            pltpu.VMEM((4, 2, 32, 1024), jnp.bfloat16),
            pltpu.VMEM((2, HEADS, 2, 32, 128), jnp.bfloat16),
            pltpu.VMEM((WIN, TOK, 128), jnp.bfloat16),
            pltpu.VMEM((WIN, 128, TOK), jnp.bfloat16),
            pltpu.VMEM((OWN, TOK, 128), jnp.bfloat16),
            pltpu.VMEM((2, KEYS, TOK, 256), jnp.float32),
            pltpu.VMEM((2, KEYS * TOK, 256), jnp.bfloat16),
            pltpu.VMEM((ZERO + 1, TOK, 128), jnp.float32),
            pltpu.VMEM((3, 2, TOK, 128), jnp.bfloat16),
            pltpu.VMEM((HALO, TOK, 128), jnp.bfloat16),
            pltpu.VMEM((HALO, TOK, 128), jnp.bfloat16),
            pltpu.VMEM((2, OWN, TOK, 128), jnp.bfloat16),
            pltpu.VMEM((HEADS, 2, 32, 128), jnp.bfloat16),
            pltpu.SMEM(partners.shape[::-1], jnp.int32),
            pltpu.SMEM((OWN, WIN), jnp.int32),
            dma((4,)),
            dma(()),
            dma((2, 16)),
            dma((2, 4)),
            dma((16,)),
            dma(()),
            dma((3,)),
            dma((3,)),
            dma((3,)),
            dma((3,)),
            dma((2, 4, 4)),
            dma((3, 4)),
            dma((3,)),
        ],
        compiler_params=pltpu.CompilerParams(collective_id=0, has_side_effects=True),
    )(query, keyed, valued, grad_out, partners.T)
    return unpacked(staged, query.shape)


def solution(mesh):
    spec = P("frames", "heads", None)
    return jax.shard_map(
        per_device,
        mesh=mesh,
        in_specs=(spec, spec, spec, spec, P()),
        out_specs=(spec,) * 4,
        check_vma=False,
    )
```

time: 45 us -> 36.4 us (0.81)
  the two profiles are of different devices: /device:TPU:385 before, /device:TPU:1 now
where the time goes in v2:
time: 36.4 us; the launch traced here: 36.3 us
  Pallas kernels  35.6 us (98%)
  between operations  0.64 us (2%)
    pallas_call x1, Pallas kernels, per_device(): pl.pallas_call(functools.partial(kernel, depth), out_shape=jax.ShapeDtype...  33.5 us
    pallas_call x1, Pallas kernels, unpacked(): pl.pallas_call(unpack_kernel, out_shape=(jax.ShapeDtypeStruct(shape, jnp....  2.16 us

profile of v2, /device:TPU:1, one launch (start us, length us, event | category | flops | bytes accessed | tf_op | source)
XLA Modules:
  0.0 36.3 jit_solution(8715169923363224008)
XLA Ops:
  0.6 33.5 %shard_map.84.staged = bf16[3,16,2,32,128]{4,3,2,1,0:T(8,128)(2,1)} custom-call(bf16[2,32,1024]{2,1,0:T(8,128)(2,1)} %q_hbm.1, bf16[2,32,1024]{2,1,0:T(8,128)(2,1)} %k_hbm.1, bf16[2,32,1024]{2,1,0:T(8,128)(2,1)} %v_hbm.1, bf16[2,32,1024]{2,1,0:T(8,128)(2,1)} %g_hbm.1, s32[6,256]{1,0:T(8,128)} %bitcast.1), custom_call_target="tpu_custom_call" | custom-call | tf_op jit(solution)/shard_map/pallas_call | solution.py:500
  34.1 2.2 %shard_map.85 = (bf16[2,32,1024]{2,1,0:T(8,128)(2,1)}, bf16[2,32,1024]{2,1,0:T(8,128)(2,1)}, bf16[2,32,1024]{2,1,0:T(8,128)(2,1)}, bf16[2,32,1024]{2,1,0:T(8,128)(2,1)}) custom-call(bf16[3,16,2,32,128]{4,3,2,1,0:T(8,128)(2,1)} %shard_map.84.staged), custom_call_target="tpu_custom_call" | custom-call | tf_op jit(solution)/shard_map/pallas_call | solution.py:63

commit v3 on v2

v3 whole, which is shorter than its diff:
```python
import functools

import jax
import jax.numpy as jnp
from jax import lax
from jax.experimental import pallas as pl
from jax.experimental.pallas import tpu as pltpu
from jax.sharding import PartitionSpec as P

HEAD_DIM = 64
SLOTS = 6
KEYS = SLOTS + 1
HALO = 6
OWN = 8
WIN = OWN + 2 * HALO
TOK = 128
HEADS = 16
ZERO = OWN * KEYS
MESH = pl.DeviceIdType.MESH
SCALE = float(HEAD_DIM) ** -0.5
OFFSETS = sorted(
    [(dx, dy) for dx in range(4) for dy in range(4)],
    key=lambda o: -(min(o[0], 4 - o[0]) + min(o[1], 4 - o[1])),
)


def turned(value):
    return jnp.concatenate([value[..., HEAD_DIM:], value[..., :HEAD_DIM]], axis=-1)


def unpack_kernel(staged, att_hbm, qg_hbm, kg_hbm, vg_hbm, taken, whole, in_sem, sem):
    low = lax.broadcasted_iota(jnp.int32, (2, 32, 128), 2) < HEAD_DIM
    outs = (qg_hbm, att_hbm, kg_hbm, vg_hbm)
    loads = []
    for kind in range(2):
        for h in range(2):
            at = (kind, slice(h * 8, (h + 1) * 8))
            loads.append(pltpu.make_async_copy(staged.at[at], taken.at[at], in_sem.at[kind, h]))
            loads[-1].start()
    copies = []
    for kind in range(2):
        for p in range(HEADS // 2):
            if p % 4 == 0:
                loads[2 * kind + p // 4].wait()
            at = slice(p * 128, (p + 1) * 128)
            even = taken[kind, 2 * p]
            odd = taken[kind, 2 * p + 1]
            whole[2 * kind, :, :, at] = jnp.where(low, even, turned(odd))
            whole[2 * kind + 1, :, :, at] = jnp.where(low, turned(even), odd)
        for i in (2 * kind, 2 * kind + 1):
            copies.append(pltpu.make_async_copy(whole.at[i], outs[i], sem.at[i]))
            copies[-1].start()
    for copy in copies:
        copy.wait()


def unpacked(staged, shape):
    return pl.pallas_call(
        unpack_kernel,
        out_shape=(jax.ShapeDtypeStruct(shape, jnp.bfloat16),) * 4,
        in_specs=[pl.BlockSpec(memory_space=pltpu.HBM)],
        out_specs=(pl.BlockSpec(memory_space=pltpu.HBM),) * 4,
        scratch_shapes=[
            pltpu.VMEM(staged.shape, jnp.bfloat16),
            pltpu.VMEM((4,) + shape, jnp.bfloat16),
            pltpu.SemaphoreType.DMA((2, 2)),
            pltpu.SemaphoreType.DMA((4,)),
        ],
    )(staged)


def kernel(
    depth,
    q_hbm,
    k_hbm,
    v_hbm,
    g_hbm,
    part_hbm,
    ostage,
    inb,
    stage,
    win,
    wint,
    own_qd,
    sc,
    pd,
    terms,
    peaks,
    cross_out,
    cross_in,
    die_out,
    die_in,
    outs,
    part,
    table,
    in_sem,
    part_sem,
    send_sem,
    kv_recv,
    qd_recv,
    halo_send,
    halo_recv,
    cross_send,
    cross_recv,
    ret_send,
    ret_recv,
    out_send,
    out_recv,
):
    fi = lax.axis_index("frames")
    y = lax.axis_index("heads")
    z = lax.div(fi, 8)
    x = lax.rem(lax.div(fi, 2), 4)
    c = lax.rem(fi, 2)
    pos = z * 2 + c
    head = y * 4 + x
    home = lax.div(x, 2)
    pair = lax.rem(x, 2) * 2 + c
    stays = home == c
    partner = fi + 1 - 2 * c
    up = jnp.where(c == 0, fi + 1, fi + 7)
    down = jnp.where(c == 1, fi - 1, fi - 7)
    has_up = pos < 2 * depth - 1
    has_down = pos > 0
    has_cross = jnp.logical_or(jnp.logical_and(c == 1, has_up), jnp.logical_and(c == 0, has_down))
    across = jnp.where(c == 0, down, up)

    loads = [
        pltpu.make_async_copy(ref, inb.at[i], in_sem.at[i])
        for i, ref in enumerate((k_hbm, v_hbm, q_hbm, g_hbm))
    ]
    for copy in loads:
        copy.start()
    part_copy = pltpu.make_async_copy(part_hbm, part, part_sem)
    part_copy.start()

    barrier = pltpu.get_barrier_semaphore()

    def greet(frame_at, head_at):
        pl.semaphore_signal(barrier, inc=1, device_id=(frame_at, head_at), device_id_type=MESH)

    for j in range(2):
        for cs in range(2):
            xs = 2 * c + j
            for dy in range(4):
                ys = lax.rem(y + dy, 4)
                if dy == 0:

                    @pl.when(jnp.logical_or(xs != x, cs != c))
                    def _():
                        greet(z * 8 + xs * 2 + cs, ys)
                else:
                    greet(z * 8 + xs * 2 + cs, ys)

    greet(partner, y)

    @pl.when(has_cross)
    def _():
        greet(across, y)

    low = lax.broadcasted_iota(jnp.int32, (2, 32, 128), 2) < HEAD_DIM

    def pack(kind, first, second, scale):
        for p in range(HEADS // 2):
            one = inb[first, :, :, p * 128 : (p + 1) * 128]
            two = inb[second, :, :, p * 128 : (p + 1) * 128]
            if scale:
                one = one * jnp.bfloat16(SCALE)
            stage[kind, 2 * p] = jnp.where(low, one, turned(two))
            stage[kind, 2 * p + 1] = jnp.where(low, turned(one), two)

    loads[0].wait()
    loads[1].wait()
    pack(0, 0, 1, False)
    loads[2].wait()
    loads[3].wait()
    pack(1, 2, 3, True)

    pl.semaphore_wait(
        barrier, 17 - stays.astype(jnp.int32) + has_cross.astype(jnp.int32)
    )

    rows = pl.ds(pl.multiple_of(y * 32, 32), 32)

    def to_slab(kind, i, act):
        dx, dy = OFFSETS[i]
        xd = lax.rem(x + dx, 4)
        yd = lax.rem(y + dy, 4)
        src = stage.at[kind, yd * 4 + xd]
        if kind == 0:
            dst = win.at[pl.ds(HALO + 2 * pair, 2), rows, :]
            landed = kv_recv.at[pair, y]
        else:
            dst = own_qd.at[pl.ds(2 * pair, 2), rows, :]
            landed = qd_recv.at[pair]
        remote = pltpu.make_async_remote_copy(
            src_ref=src,
            dst_ref=dst,
            send_sem=send_sem.at[kind, i],
            recv_sem=landed,
            device_id=(z * 8 + xd * 2 + home, yd),
            device_id_type=MESH,
        )
        if dx == 0 and dy == 0:
            if act == "start":
                local = pltpu.make_async_copy(src, dst, landed)
                pl.when(stays)(local.start)
                pl.when(jnp.logical_not(stays))(remote.start)
            else:
                pl.when(jnp.logical_not(stays))(remote.wait_send)
        elif act == "start":
            remote.start()
        else:
            remote.wait_send()

    for i in range(16):
        to_slab(0, i, "start")

    for i in range(16):
        to_slab(1, i, "start")

    far = jnp.where(c == 0, 0, HALO + OWN)

    @pl.when(jnp.logical_not(has_cross))
    def _():
        win[pl.ds(far, HALO)] = jnp.zeros((HALO, TOK, 128), jnp.bfloat16)
        cross_in[...] = jnp.zeros_like(cross_in)

    def byte_wait(ref, sem):
        pltpu.make_async_copy(ref, ref, sem).wait()

    def flip(w):
        wint[w] = win[w].T

    passed = []
    for n, dy in enumerate((2, 1, 3, 0)):
        ys = lax.rem(y + dy, 4)
        some = pl.ds(pl.multiple_of(ys * 32, 32), 32)
        for k in (1, 2, 0, 3):
            here = win.at[HALO + 2 * k : HALO + 2 * k + 2, some, :]
            byte_wait(here, kv_recv.at[k, ys])
            for side, land in ((0, 2 * k - 2), (1, HALO + OWN + 2 * k)):
                if k == (0, 3)[side]:
                    continue
                copy = pltpu.make_async_remote_copy(
                    src_ref=here,
                    dst_ref=win.at[land : land + 2, some, :],
                    send_sem=halo_send.at[side, k - 1 + side, n],
                    recv_sem=halo_recv.at[side],
                    device_id=((up, down)[side], y),
                    device_id_type=MESH,
                )
                pl.when((has_up, has_down)[side])(copy.start)
                passed.append((side, copy))
    part_copy.wait()

    base = pos * OWN - HALO

    def turned_frame(i):
        return jnp.where(c == 0, i, OWN - 1 - i)

    @pl.loop(0, OWN)
    def _(i):
        f = turned_frame(i)
        at_frame = pos * OWN + f
        for w in range(WIN):
            target = base + jnp.where(c == 0, w, WIN - 1 - w)
            at = jnp.int32(ZERO)
            for s in range(SLOTS):
                at = jnp.where(part[s, at_frame] == target, i * KEYS + 1 + s, at)
            table[i, w] = jnp.where(i + HALO == w, i * KEYS, at)

    terms[ZERO] = jnp.zeros((TOK, 128), jnp.float32)
    for f in range(OWN):
        flip(HALO + f)
    for k in range(4):
        byte_wait(own_qd.at[2 * k : 2 * k + 2], qd_recv.at[k])

    @pl.when(has_down)
    def _():
        byte_wait(win.at[:HALO], halo_recv.at[0])

    @pl.when(has_up)
    def _():
        byte_wait(win.at[HALO + OWN :], halo_recv.at[1])

    for w in range(HALO):
        flip(w)
        flip(HALO + OWN + w)

    half = lax.broadcasted_iota(jnp.int32, (TOK, 128), 1) < HEAD_DIM

    def slots_of(i):
        f = turned_frame(i)
        at = [f + HALO]
        bias = [None]
        for s in range(SLOTS):
            listed = part[s, pos * OWN + f]
            close = jnp.minimum(jnp.maximum(listed - base, 0), WIN - 1)
            at.append(jnp.where(listed >= 0, close, f + HALO))
            bias.append(jnp.where(listed >= 0, jnp.float32(0.0), jnp.float32(-jnp.inf)))
        return f, at, bias

    def block_diagonal(f):
        mixed = own_qd[f]
        none = jnp.zeros_like(mixed)
        return jnp.concatenate([jnp.where(half, none, mixed), jnp.where(half, mixed, none)], axis=0)

    def products(i):
        u = i % 2
        f, at, bias = slots_of(i)
        keyed = jnp.concatenate([win[at[s]] for s in range(KEYS)], axis=0)
        both = lax.dot_general(
            keyed, block_diagonal(f), (((1,), (1,)), ((), ())), preferred_element_type=jnp.float32
        )
        top = None
        for s in range(KEYS):
            here = both[s * TOK : (s + 1) * TOK]
            score = here[:, 128:]
            if bias[s] is not None:
                score = score + bias[s]
            sc[u, s, :, :128] = here[:, :128]
            sc[u, s, :, 128:] = score
            most = jnp.max(score.reshape(16, 8, 128), axis=0)
            top = most if top is None else jnp.maximum(top, most)
        peaks[u] = top

    def exponentials(i):
        u = i % 2
        peak = jnp.max(peaks[u], axis=0, keepdims=True)
        total = jnp.zeros((8, 128), jnp.float32)
        dsum = jnp.zeros((8, 128), jnp.float32)
        for s in range(KEYS):
            e = jnp.exp(sc[u, s, :, 128:] - peak)
            sc[u, s, :, 128:] = e
            total = total + jnp.sum(e.reshape(16, 8, 128), axis=0)
            dsum = dsum + jnp.sum((e * sc[u, s, :, :128]).reshape(16, 8, 128), axis=0)
        inv = 1.0 / jnp.sum(total, axis=0, keepdims=True)
        return inv, jnp.sum(dsum, axis=0, keepdims=True) * inv

    def gradients(i, inv, delta):
        u = i % 2
        for s in range(KEYS):
            w = sc[u, s, :, 128:] * inv
            rows_at = slice(s * TOK, (s + 1) * TOK)
            pd[u, rows_at, :128] = w.astype(jnp.bfloat16)
            pd[u, rows_at, 128:] = (w * (sc[u, s, :, :128] - delta)).astype(jnp.bfloat16)

    def key_terms(i):
        u = i % 2
        prod = jnp.dot(pd[u], block_diagonal(turned_frame(i)), preferred_element_type=jnp.float32)
        for s in range(KEYS):
            terms[i * KEYS + s] = prod[s * TOK : (s + 1) * TOK]

    def query_terms(i):
        u = i % 2
        f, at, _ = slots_of(i)
        turned_kv = jnp.concatenate([wint[at[s]] for s in range(KEYS)], axis=1)
        res = jnp.dot(turned_kv, pd[u], preferred_element_type=jnp.float32)
        outcome = jnp.concatenate([res[:HEAD_DIM, 128:] * SCALE, res[HEAD_DIM:, :128]], axis=0)
        outs[0, f] = outcome.T.astype(jnp.bfloat16)

    def gathered(w):
        total = None
        for i in range(max(0, w - 2 * HALO), min(OWN, w + 1)):
            term = terms[table[i, w]]
            total = term if total is None else total + term
        return total

    def pair_of(j):
        return jnp.where(c == 0, j, 3 - j)

    def give_back(kind, j, act):
        k = pair_of(j)
        xs = 2 * c + lax.div(k, 2)
        cs = lax.rem(k, 2)
        for dy in range(4):
            ys = lax.rem(y + (2, 1, 3, 0)[dy], 4)
            src = outs.at[kind, pl.ds(2 * k, 2), pl.ds(pl.multiple_of(ys * 32, 32), 32), :]
            dst = ostage.at[kind, head]
            remote = pltpu.make_async_remote_copy(
                src_ref=src,
                dst_ref=dst,
                send_sem=out_send.at[kind, j, dy],
                recv_sem=out_recv.at[kind],
                device_id=(z * 8 + xs * 2 + cs, ys),
                device_id_type=MESH,
            )
            if dy == 3:
                mine = jnp.logical_and(xs == x, cs == c)
                if act == "start":
                    local = pltpu.make_async_copy(src, dst, out_recv.at[kind])
                    pl.when(mine)(local.start)
                    pl.when(jnp.logical_not(mine))(remote.start)
                else:
                    pl.when(jnp.logical_not(mine))(remote.wait_send)
            elif act == "start":
                remote.start()
            else:
                remote.wait_send()

    cross_copies = [
        pltpu.make_async_remote_copy(
            src_ref=cross_out.at[2 * j : 2 * j + 2],
            dst_ref=cross_in.at[2 * j : 2 * j + 2],
            send_sem=cross_send.at[j],
            recv_sem=cross_recv.at[j],
            device_id=(across, y),
            device_id_type=MESH,
        )
        for j in range(3)
    ]

    products(0)
    for i in range(OWN + 1):
        if i + 1 < OWN:
            products(i + 1)
        if i < OWN:
            inv, delta = exponentials(i)
        if i > 0:
            key_terms(i - 1)
        if i < OWN:
            gradients(i, inv, delta)
        if i > 0:
            query_terms(i - 1)
        if i > 0 and i % 2 == 0:
            j = i // 2 - 1
            if j < 3:
                for w in (2 * j, 2 * j + 1):
                    cross_out[w] = gathered(w).astype(jnp.bfloat16)
                pl.when(has_cross)(cross_copies[j].start)
            give_back(0, j, "start")

    ret_copies = []
    for j in range(3):
        for q in (2 * j, 2 * j + 1):
            die_out[q] = gathered(HALO + OWN + q).astype(jnp.bfloat16)
        copy = pltpu.make_async_remote_copy(
            src_ref=die_out.at[2 * j : 2 * j + 2],
            dst_ref=die_in.at[2 * j : 2 * j + 2],
            send_sem=ret_send.at[j],
            recv_sem=ret_recv.at[j],
            device_id=(partner, y),
            device_id_type=MESH,
        )
        copy.start()
        ret_copies.append(copy)
    for j in (0, 3, 2, 1):
        sums = [gathered(HALO + i) for i in (2 * j, 2 * j + 1)]
        if j < 3:
            pl.when(has_cross)(cross_copies[2 - j].wait_recv)
        if j > 0:
            ret_copies[3 - j].wait_recv()
        for n, i in enumerate((2 * j, 2 * j + 1)):
            total = sums[n]
            if i < HALO:
                total = total + cross_in[HALO - 1 - i].astype(jnp.float32)
            if j > 0:
                total = total + die_in[OWN - 1 - i].astype(jnp.float32)
            outs[1, turned_frame(i)] = total.astype(jnp.bfloat16)
        give_back(1, j, "start")

    for i in range(16):
        to_slab(0, i, "wait")
        to_slab(1, i, "wait")
    for side, copy in passed:
        pl.when((has_up, has_down)[side])(copy.wait_send)
    for copy in cross_copies:
        pl.when(has_cross)(copy.wait_send)
    for copy in ret_copies:
        copy.wait_send()
    for j in range(4):
        give_back(0, j, "wait")
        give_back(1, j, "wait")
    for kind in range(2):
        byte_wait(ostage.at[kind], out_recv.at[kind])


def per_device(query, keyed, valued, grad_out, partners):
    depth = lax.axis_size("frames") // 8
    dma = pltpu.SemaphoreType.DMA
    staged = pl.pallas_call(
        functools.partial(kernel, depth),
        out_shape=jax.ShapeDtypeStruct((2, HEADS, 2, 32, 128), jnp.bfloat16),
        in_specs=[pl.BlockSpec(memory_space=pltpu.HBM)] * 5,
        out_specs=pl.BlockSpec(memory_space=pltpu.HBM),
        scratch_shapes=[
            pltpu.VMEM((4, 2, 32, 1024), jnp.bfloat16),
            pltpu.VMEM((2, HEADS, 2, 32, 128), jnp.bfloat16),
            pltpu.VMEM((WIN, TOK, 128), jnp.bfloat16),
            pltpu.VMEM((WIN, 128, TOK), jnp.bfloat16),
            pltpu.VMEM((OWN, TOK, 128), jnp.bfloat16),
            pltpu.VMEM((2, KEYS, TOK, 256), jnp.float32),
            pltpu.VMEM((2, KEYS * TOK, 256), jnp.bfloat16),
            pltpu.VMEM((ZERO + 1, TOK, 128), jnp.float32),
            pltpu.VMEM((2, 8, 128), jnp.float32),
            pltpu.VMEM((HALO, TOK, 128), jnp.bfloat16),
            pltpu.VMEM((HALO, TOK, 128), jnp.bfloat16),
            pltpu.VMEM((HALO, TOK, 128), jnp.bfloat16),
            pltpu.VMEM((HALO, TOK, 128), jnp.bfloat16),
            pltpu.VMEM((2, OWN, TOK, 128), jnp.bfloat16),
            pltpu.SMEM(partners.shape[::-1], jnp.int32),
            pltpu.SMEM((OWN, WIN), jnp.int32),
            dma((4,)),
            dma(()),
            dma((2, 16)),
            dma((4, 4)),
            dma((4,)),
            dma((2, 3, 4)),
            dma((2,)),
            dma((3,)),
            dma((3,)),
            dma((3,)),
            dma((3,)),
            dma((2, 4, 4)),
            dma((2,)),
        ],
        compiler_params=pltpu.CompilerParams(collective_id=0, has_side_effects=True),
    )(query, keyed, valued, grad_out, partners.T)
    return unpacked(staged, query.shape)


def solution(mesh):
    spec = P("frames", "heads", None)
    return jax.shard_map(
        per_device,
        mesh=mesh,
        in_specs=(spec, spec, spec, spec, P()),
        out_specs=(spec,) * 4,
        check_vma=False,
    )
```

time: 36.4 us -> 34.9 us (0.959)
  the two profiles are of different devices: /device:TPU:1 before, /device:TPU:129 now
where the time goes in v3:
time: 34.9 us; the launch traced here: 34.7 us
  Pallas kernels  34.1 us (98%)
  between operations  0.64 us (2%)
    pallas_call x1, Pallas kernels, per_device(): pl.pallas_call(functools.partial(kernel, depth), out_shape=jax.ShapeDtype...  32 us
    pallas_call x1, Pallas kernels, unpacked(): pl.pallas_call(unpack_kernel, out_shape=(jax.ShapeDtypeStruct(shape, jnp....  2.1 us

profile of v3, /device:TPU:129, one launch (start us, length us, event | category | flops | bytes accessed | tf_op | source)
XLA Modules:
  0.0 34.7 jit_solution(10369027773681007733)
XLA Ops:
  0.6 32.0 %shard_map.84.staged = bf16[2,16,2,32,128]{4,3,2,1,0:T(8,128)(2,1)} custom-call(bf16[2,32,1024]{2,1,0:T(8,128)(2,1)} %q_hbm.1, bf16[2,32,1024]{2,1,0:T(8,128)(2,1)} %k_hbm.1, bf16[2,32,1024]{2,1,0:T(8,128)(2,1)} %v_hbm.1, bf16[2,32,1024]{2,1,0:T(8,128)(2,1)} %g_hbm.1, s32[6,256]{1,0:T(8,128)} %bitcast.1), custom_call_target="tpu_custom_call" | custom-call | tf_op jit(solution)/shard_map/pallas_call | solution.py:482
  32.6 2.1 %shard_map.85 = (bf16[2,32,1024]{2,1,0:T(8,128)(2,1)}, bf16[2,32,1024]{2,1,0:T(8,128)(2,1)}, bf16[2,32,1024]{2,1,0:T(8,128)(2,1)}, bf16[2,32,1024]{2,1,0:T(8,128)(2,1)}) custom-call(bf16[2,16,2,32,128]{4,3,2,1,0:T(8,128)(2,1)} %shard_map.84.staged), custom_call_target="tpu_custom_call" | custom-call | tf_op jit(solution)/shard_map/pallas_call | solution.py:58

commit v4 on v3

--- a/solution.py
+++ b/solution.py
@@ -17,6 +17,7 @@
 HEADS = 16
 ZERO = OWN * KEYS
 MESH = pl.DeviceIdType.MESH
+ORDER = (6, 0, 1, 2, 3, 4, 5, 7)
 SCALE = float(HEAD_DIM) ** -0.5
 OFFSETS = sorted(
     [(dx, dy) for dx in range(4) for dy in range(4)],
@@ -28,20 +29,12 @@
     return jnp.concatenate([value[..., HEAD_DIM:], value[..., :HEAD_DIM]], axis=-1)
 
 
-def unpack_kernel(staged, att_hbm, qg_hbm, kg_hbm, vg_hbm, taken, whole, in_sem, sem):
+def unpack_kernel(taken, att_hbm, qg_hbm, kg_hbm, vg_hbm, whole, sem):
     low = lax.broadcasted_iota(jnp.int32, (2, 32, 128), 2) < HEAD_DIM
     outs = (qg_hbm, att_hbm, kg_hbm, vg_hbm)
-    loads = []
-    for kind in range(2):
-        for h in range(2):
-            at = (kind, slice(h * 8, (h + 1) * 8))
-            loads.append(pltpu.make_async_copy(staged.at[at], taken.at[at], in_sem.at[kind, h]))
-            loads[-1].start()
     copies = []
     for kind in range(2):
         for p in range(HEADS // 2):
-            if p % 4 == 0:
-                loads[2 * kind + p // 4].wait()
             at = slice(p * 128, (p + 1) * 128)
             even = taken[kind, 2 * p]
             odd = taken[kind, 2 * p + 1]
@@ -58,14 +51,13 @@
     return pl.pallas_call(
         unpack_kernel,
         out_shape=(jax.ShapeDtypeStruct(shape, jnp.bfloat16),) * 4,
-        in_specs=[pl.BlockSpec(memory_space=pltpu.HBM)],
+        in_specs=[pl.BlockSpec(memory_space=pltpu.VMEM)],
         out_specs=(pl.BlockSpec(memory_space=pltpu.HBM),) * 4,
         scratch_shapes=[
-            pltpu.VMEM(staged.shape, jnp.bfloat16),
             pltpu.VMEM((4,) + shape, jnp.bfloat16),
-            pltpu.SemaphoreType.DMA((2, 2)),
             pltpu.SemaphoreType.DMA((4,)),
         ],
+        compiler_params=pltpu.CompilerParams(vmem_limit_bytes=16 * 2**20),
     )(staged)
 
 
@@ -80,6 +72,7 @@
     inb,
     stage,
     win,
+    far_land,
     wint,
     own_qd,
     sc,
@@ -142,7 +135,7 @@
     for j in range(2):
         for cs in range(2):
             xs = 2 * c + j
-            for dy in range(4):
+            for dy in (2, 1, 3, 0):
                 ys = lax.rem(y + dy, 4)
                 if dy == 0:
 
@@ -172,9 +165,6 @@
     loads[0].wait()
     loads[1].wait()
     pack(0, 0, 1, False)
-    loads[2].wait()
-    loads[3].wait()
-    pack(1, 2, 3, True)
 
     pl.semaphore_wait(
         barrier, 17 - stays.astype(jnp.int32) + has_cross.astype(jnp.int32)
@@ -216,6 +206,9 @@
     for i in range(16):
         to_slab(0, i, "start")
 
+    loads[2].wait()
+    loads[3].wait()
+    pack(1, 2, 3, True)
     for i in range(16):
         to_slab(1, i, "start")
 
@@ -223,7 +216,7 @@
 
     @pl.when(jnp.logical_not(has_cross))
     def _():
-        win[pl.ds(far, HALO)] = jnp.zeros((HALO, TOK, 128), jnp.bfloat16)
+        far_land[...] = jnp.zeros_like(far_land)
         cross_in[...] = jnp.zeros_like(cross_in)
 
     def byte_wait(ref, sem):
@@ -239,19 +232,33 @@
         for k in (1, 2, 0, 3):
             here = win.at[HALO + 2 * k : HALO + 2 * k + 2, some, :]
             byte_wait(here, kv_recv.at[k, ys])
-            for side, land in ((0, 2 * k - 2), (1, HALO + OWN + 2 * k)):
-                if k == (0, 3)[side]:
-                    continue
-                copy = pltpu.make_async_remote_copy(
-                    src_ref=here,
-                    dst_ref=win.at[land : land + 2, some, :],
-                    send_sem=halo_send.at[side, k - 1 + side, n],
-                    recv_sem=halo_recv.at[side],
-                    device_id=((up, down)[side], y),
-                    device_id_type=MESH,
-                )
-                pl.when((has_up, has_down)[side])(copy.start)
-                passed.append((side, copy))
+            to_partner = pltpu.make_async_remote_copy(
+                src_ref=here,
+                dst_ref=win.at[pl.ds(jnp.where(c == 0, 2 * k - 2, HALO + OWN + 2 * k), 2), some, :],
+                send_sem=halo_send.at[0, k, n],
+                recv_sem=halo_recv.at[0],
+                device_id=(partner, y),
+                device_id_type=MESH,
+            )
+            to_across = pltpu.make_async_remote_copy(
+                src_ref=here,
+                dst_ref=far_land.at[pl.ds(jnp.where(c == 0, 2 * k, 2 * k - 2), 2), some, :],
+                send_sem=halo_send.at[1, k, n],
+                recv_sem=halo_recv.at[1],
+                device_id=(across, y),
+                device_id_type=MESH,
+            )
+            if k in (1, 2):
+                crossing = has_cross
+                to_partner.start()
+                passed.append((None, to_partner))
+            else:
+                staying = (c == 1) if k == 0 else (c == 0)
+                crossing = jnp.logical_and(has_cross, jnp.logical_not(staying))
+                pl.when(staying)(to_partner.start)
+                passed.append((staying, to_partner))
+            pl.when(crossing)(to_across.start)
+            passed.append((crossing, to_across))
     part_copy.wait()
 
     base = pos * OWN - HALO
@@ -276,17 +283,10 @@
     for k in range(4):
         byte_wait(own_qd.at[2 * k : 2 * k + 2], qd_recv.at[k])
 
-    @pl.when(has_down)
-    def _():
-        byte_wait(win.at[:HALO], halo_recv.at[0])
-
-    @pl.when(has_up)
-    def _():
-        byte_wait(win.at[HALO + OWN :], halo_recv.at[1])
-
+    near = jnp.where(c == 0, HALO + OWN, 0)
+    byte_wait(win.at[pl.ds(near, HALO)], halo_recv.at[0])
     for w in range(HALO):
-        flip(w)
-        flip(HALO + OWN + w)
+        flip(near + w)
 
     half = lax.broadcasted_iota(jnp.int32, (TOK, 128), 1) < HEAD_DIM
 
@@ -306,9 +306,9 @@
         none = jnp.zeros_like(mixed)
         return jnp.concatenate([jnp.where(half, none, mixed), jnp.where(half, mixed, none)], axis=0)
 
-    def products(i):
-        u = i % 2
-        f, at, bias = slots_of(i)
+    def products(n):
+        u = n % 2
+        f, at, bias = slots_of(ORDER[n])
         keyed = jnp.concatenate([win[at[s]] for s in range(KEYS)], axis=0)
         both = lax.dot_general(
             keyed, block_diagonal(f), (((1,), (1,)), ((), ())), preferred_element_type=jnp.float32
@@ -325,8 +325,8 @@
             top = most if top is None else jnp.maximum(top, most)
         peaks[u] = top
 
-    def exponentials(i):
-        u = i % 2
+    def exponentials(n):
+        u = n % 2
         peak = jnp.max(peaks[u], axis=0, keepdims=True)
         total = jnp.zeros((8, 128), jnp.float32)
         dsum = jnp.zeros((8, 128), jnp.float32)
@@ -338,23 +338,23 @@
         inv = 1.0 / jnp.sum(total, axis=0, keepdims=True)
         return inv, jnp.sum(dsum, axis=0, keepdims=True) * inv
 
-    def gradients(i, inv, delta):
-        u = i % 2
+    def gradients(n, inv, delta):
+        u = n % 2
         for s in range(KEYS):
             w = sc[u, s, :, 128:] * inv
             rows_at = slice(s * TOK, (s + 1) * TOK)
             pd[u, rows_at, :128] = w.astype(jnp.bfloat16)
             pd[u, rows_at, 128:] = (w * (sc[u, s, :, :128] - delta)).astype(jnp.bfloat16)
 
-    def key_terms(i):
-        u = i % 2
-        prod = jnp.dot(pd[u], block_diagonal(turned_frame(i)), preferred_element_type=jnp.float32)
+    def key_terms(n):
+        u = n % 2
+        prod = jnp.dot(pd[u], block_diagonal(turned_frame(ORDER[n])), preferred_element_type=jnp.float32)
         for s in range(KEYS):
-            terms[i * KEYS + s] = prod[s * TOK : (s + 1) * TOK]
-
-    def query_terms(i):
-        u = i % 2
-        f, at, _ = slots_of(i)
+            terms[ORDER[n] * KEYS + s] = prod[s * TOK : (s + 1) * TOK]
+
+    def query_terms(n):
+        u = n % 2
+        f, at, _ = slots_of(ORDER[n])
         turned_kv = jnp.concatenate([wint[at[s]] for s in range(KEYS)], axis=1)
         res = jnp.dot(turned_kv, pd[u], preferred_element_type=jnp.float32)
         outcome = jnp.concatenate([res[:HEAD_DIM, 128:] * SCALE, res[HEAD_DIM:, :128]], axis=0)
@@ -412,19 +412,28 @@
     ]
 
     products(0)
-    for i in range(OWN + 1):
-        if i + 1 < OWN:
-            products(i + 1)
-        if i < OWN:
-            inv, delta = exponentials(i)
-        if i > 0:
-            key_terms(i - 1)
-        if i < OWN:
-            gradients(i, inv, delta)
-        if i > 0:
-            query_terms(i - 1)
-        if i > 0 and i % 2 == 0:
-            j = i // 2 - 1
+
+    @pl.when(has_cross)
+    def _():
+        byte_wait(far_land, halo_recv.at[1])
+
+    for w in range(HALO):
+        win[far + w] = far_land[w]
+        wint[far + w] = far_land[w].T
+
+    for n in range(OWN + 1):
+        if n + 1 < OWN:
+            products(n + 1)
+        if n < OWN:
+            inv, delta = exponentials(n)
+        if n > 0:
+            key_terms(n - 1)
+        if n < OWN:
+            gradients(n, inv, delta)
+        if n > 0:
+            query_terms(n - 1)
+        if n in (3, 5, 7, 8):
+            j = (3, 5, 7, 8).index(n)
             if j < 3:
                 for w in (2 * j, 2 * j + 1):
                     cross_out[w] = gathered(w).astype(jnp.bfloat16)
@@ -445,7 +454,7 @@
         )
         copy.start()
         ret_copies.append(copy)
-    for j in (0, 3, 2, 1):
+    for j in (3, 2, 1, 0):
         sums = [gathered(HALO + i) for i in (2 * j, 2 * j + 1)]
         if j < 3:
             pl.when(has_cross)(cross_copies[2 - j].wait_recv)
@@ -463,8 +472,11 @@
     for i in range(16):
         to_slab(0, i, "wait")
         to_slab(1, i, "wait")
-    for side, copy in passed:
-        pl.when((has_up, has_down)[side])(copy.wait_send)
+    for wanted, copy in passed:
+        if wanted is None:
+            copy.wait_send()
+        else:
+            pl.when(wanted)(copy.wait_send)
     for copy in cross_copies:
         pl.when(has_cross)(copy.wait_send)
     for copy in ret_copies:
@@ -481,13 +493,14 @@
     dma = pltpu.SemaphoreType.DMA
     staged = pl.pallas_call(
         functools.partial(kernel, depth),
-        out_shape=jax.ShapeDtypeStruct((2, HEADS, 2, 32, 128), jnp.bfloat16),
+        out_shape=pltpu.VMEM((2, HEADS, 2, 32, 128), jnp.bfloat16),
         in_specs=[pl.BlockSpec(memory_space=pltpu.HBM)] * 5,
-        out_specs=pl.BlockSpec(memory_space=pltpu.HBM),
+        out_specs=pl.BlockSpec(memory_space=pltpu.VMEM),
         scratch_shapes=[
             pltpu.VMEM((4, 2, 32, 1024), jnp.bfloat16),
             pltpu.VMEM((2, HEADS, 2, 32, 128), jnp.bfloat16),
             pltpu.VMEM((WIN, TOK, 128), jnp.bfloat16),
+            pltpu.VMEM((HALO, TOK, 128), jnp.bfloat16),
             pltpu.VMEM((WIN, 128, TOK), jnp.bfloat16),
             pltpu.VMEM((OWN, TOK, 128), jnp.bfloat16),
             pltpu.VMEM((2, KEYS, TOK, 256), jnp.float32),
@@ -506,7 +519,7 @@
             dma((2, 16)),
             dma((4, 4)),
             dma((4,)),
-            dma((2, 3, 4)),
+            dma((2, 4, 4)),
             dma((2,)),
             dma((3,)),
             dma((3,)),
@@ -515,7 +528,7 @@
             dma((2, 4, 4)),
             dma((2,)),
         ],
-        compiler_params=pltpu.CompilerParams(collective_id=0, has_side_effects=True),
+        compiler_params=pltpu.CompilerParams(collective_id=0, has_side_effects=True, vmem_limit_bytes=60 * 2**20),
     )(query, keyed, valued, grad_out, partners.T)
     return unpacked(staged, query.shape)
 

time: 34.9 us -> 33.3 us (0.954)
  the two profiles are of different devices: /device:TPU:129 before, /device:TPU:96 now
where the time goes in v4:
time: 33.3 us; the launch traced here: 33.2 us
  Pallas kernels  32.5 us (98%)
  between operations  0.64 us (2%)
    pallas_call x1, Pallas kernels, per_device(): pl.pallas_call(functools.partial(kernel, depth), out_shape=pltpu.VMEM((2,...  31.6 us
    pallas_call x1, Pallas kernels, unpacked(): pl.pallas_call(unpack_kernel, out_shape=(jax.ShapeDtypeStruct(shape, jnp....  0.96 us

profile of v4, /device:TPU:96, one launch (start us, length us, event | category | flops | bytes accessed | tf_op | source)
XLA Modules:
  0.0 33.2 jit_solution(16822115893040538541)
XLA Ops:
  0.6 31.6 %shard_map.84.taken = bf16[2,16,2,32,128]{4,3,2,1,0:T(8,128)(2,1)S(1)} custom-call(bf16[2,32,1024]{2,1,0:T(8,128)(2,1)} %q_hbm.1, bf16[2,32,1024]{2,1,0:T(8,128)(2,1)} %k_hbm.1, bf16[2,32,1024]{2,1,0:T(8,128)(2,1)} %v_hbm.1, bf16[2,32,1024]{2,1,0:T(8,128)(2,1)} %g_hbm.1, s32[6,256]{1,0:T(8,128)} %bitcast.1), custom_call_target="tpu_custom_call" | custom-call | tf_op jit(solution)/shard_map/pallas_call | solution.py:494
  32.2 1.0 %shard_map.85 = (bf16[2,32,1024]{2,1,0:T(8,128)(2,1)}, bf16[2,32,1024]{2,1,0:T(8,128)(2,1)}, bf16[2,32,1024]{2,1,0:T(8,128)(2,1)}, bf16[2,32,1024]{2,1,0:T(8,128)(2,1)}) custom-call(bf16[2,16,2,32,128]{4,3,2,1,0:T(8,128)(2,1)S(1)} %shard_map.84.taken), custom_call_target="tpu_custom_call" | custom-call | tf_op jit(solution)/shard_map/pallas_call | solution.py:51

commit v5 on v4

--- a/solution.py
+++ b/solution.py
@@ -179,7 +179,7 @@
         src = stage.at[kind, yd * 4 + xd]
         if kind == 0:
             dst = win.at[pl.ds(HALO + 2 * pair, 2), rows, :]
-            landed = kv_recv.at[pair, y]
+            landed = kv_recv.at[pair]
         else:
             dst = own_qd.at[pl.ds(2 * pair, 2), rows, :]
             landed = qd_recv.at[pair]
@@ -226,39 +226,36 @@
         wint[w] = win[w].T
 
     passed = []
-    for n, dy in enumerate((2, 1, 3, 0)):
-        ys = lax.rem(y + dy, 4)
-        some = pl.ds(pl.multiple_of(ys * 32, 32), 32)
-        for k in (1, 2, 0, 3):
-            here = win.at[HALO + 2 * k : HALO + 2 * k + 2, some, :]
-            byte_wait(here, kv_recv.at[k, ys])
-            to_partner = pltpu.make_async_remote_copy(
-                src_ref=here,
-                dst_ref=win.at[pl.ds(jnp.where(c == 0, 2 * k - 2, HALO + OWN + 2 * k), 2), some, :],
-                send_sem=halo_send.at[0, k, n],
-                recv_sem=halo_recv.at[0],
-                device_id=(partner, y),
-                device_id_type=MESH,
-            )
-            to_across = pltpu.make_async_remote_copy(
-                src_ref=here,
-                dst_ref=far_land.at[pl.ds(jnp.where(c == 0, 2 * k, 2 * k - 2), 2), some, :],
-                send_sem=halo_send.at[1, k, n],
-                recv_sem=halo_recv.at[1],
-                device_id=(across, y),
-                device_id_type=MESH,
-            )
-            if k in (1, 2):
-                crossing = has_cross
-                to_partner.start()
-                passed.append((None, to_partner))
-            else:
-                staying = (c == 1) if k == 0 else (c == 0)
-                crossing = jnp.logical_and(has_cross, jnp.logical_not(staying))
-                pl.when(staying)(to_partner.start)
-                passed.append((staying, to_partner))
-            pl.when(crossing)(to_across.start)
-            passed.append((crossing, to_across))
+    for k in (1, 2, 0, 3):
+        here = win.at[HALO + 2 * k : HALO + 2 * k + 2]
+        byte_wait(here, kv_recv.at[k])
+        to_partner = pltpu.make_async_remote_copy(
+            src_ref=here,
+            dst_ref=win.at[pl.ds(jnp.where(c == 0, 2 * k - 2, HALO + OWN + 2 * k), 2)],
+            send_sem=halo_send.at[0, k],
+            recv_sem=halo_recv.at[0],
+            device_id=(partner, y),
+            device_id_type=MESH,
+        )
+        to_across = pltpu.make_async_remote_copy(
+            src_ref=here,
+            dst_ref=far_land.at[pl.ds(jnp.where(c == 0, 2 * k, 2 * k - 2), 2)],
+            send_sem=halo_send.at[1, k],
+            recv_sem=halo_recv.at[1],
+            device_id=(across, y),
+            device_id_type=MESH,
+        )
+        if k in (1, 2):
+            crossing = has_cross
+            to_partner.start()
+            passed.append((None, to_partner))
+        else:
+            staying = (c == 1) if k == 0 else (c == 0)
+            crossing = jnp.logical_and(has_cross, jnp.logical_not(staying))
+            pl.when(staying)(to_partner.start)
+            passed.append((staying, to_partner))
+        pl.when(crossing)(to_across.start)
+        passed.append((crossing, to_across))
     part_copy.wait()
 
     base = pos * OWN - HALO
@@ -517,9 +514,9 @@
             dma((4,)),
             dma(()),
             dma((2, 16)),
-            dma((4, 4)),
             dma((4,)),
-            dma((2, 4, 4)),
+            dma((4,)),
+            dma((2, 4)),
             dma((2,)),
             dma((3,)),
             dma((3,)),

time: 33.3 us -> 32.9 us (0.988)
  the two profiles are of different devices: /device:TPU:96 before, /device:TPU:224 now
where the time goes in v5:
time: 32.9 us; the launch traced here: 32.8 us
  Pallas kernels  32.1 us (98%)
  between operations  0.64 us (2%)
    pallas_call x1, Pallas kernels, per_device(): pl.pallas_call(functools.partial(kernel, depth), out_shape=pltpu.VMEM((2,...  31.2 us
    pallas_call x1, Pallas kernels, unpacked(): pl.pallas_call(unpack_kernel, out_shape=(jax.ShapeDtypeStruct(shape, jnp....  0.96 us

profile of v5, /device:TPU:224, one launch (start us, length us, event | category | flops | bytes accessed | tf_op | source)
XLA Modules:
  0.0 32.8 jit_solution(1471596167939496220)
XLA Ops:
  0.6 31.2 %shard_map.84.taken = bf16[2,16,2,32,128]{4,3,2,1,0:T(8,128)(2,1)S(1)} custom-call(bf16[2,32,1024]{2,1,0:T(8,128)(2,1)} %q_hbm.1, bf16[2,32,1024]{2,1,0:T(8,128)(2,1)} %k_hbm.1, bf16[2,32,1024]{2,1,0:T(8,128)(2,1)} %v_hbm.1, bf16[2,32,1024]{2,1,0:T(8,128)(2,1)} %g_hbm.1, s32[6,256]{1,0:T(8,128)} %bitcast.1), custom_call_target="tpu_custom_call" | custom-call | tf_op jit(solution)/shard_map/pallas_call | solution.py:491
  31.8 1.0 %shard_map.85 = (bf16[2,32,1024]{2,1,0:T(8,128)(2,1)}, bf16[2,32,1024]{2,1,0:T(8,128)(2,1)}, bf16[2,32,1024]{2,1,0:T(8,128)(2,1)}, bf16[2,32,1024]{2,1,0:T(8,128)(2,1)}) custom-call(bf16[2,16,2,32,128]{4,3,2,1,0:T(8,128)(2,1)S(1)} %shard_map.84.taken), custom_call_target="tpu_custom_call" | custom-call | tf_op jit(solution)/shard_map/pallas_call | solution.py:51

commit v6 on v5

--- a/solution.py
+++ b/solution.py
@@ -79,6 +79,7 @@
     pd,
     terms,
     peaks,
+    acc,
     cross_out,
     cross_in,
     die_out,
@@ -451,8 +452,10 @@
         )
         copy.start()
         ret_copies.append(copy)
+    for i in range(OWN):
+        acc[i] = gathered(HALO + i)
     for j in (3, 2, 1, 0):
-        sums = [gathered(HALO + i) for i in (2 * j, 2 * j + 1)]
+        sums = [acc[i] for i in (2 * j, 2 * j + 1)]
         if j < 3:
             pl.when(has_cross)(cross_copies[2 - j].wait_recv)
         if j > 0:
@@ -504,6 +507,7 @@
             pltpu.VMEM((2, KEYS * TOK, 256), jnp.bfloat16),
             pltpu.VMEM((ZERO + 1, TOK, 128), jnp.float32),
             pltpu.VMEM((2, 8, 128), jnp.float32),
+            pltpu.VMEM((OWN, TOK, 128), jnp.float32),
             pltpu.VMEM((HALO, TOK, 128), jnp.bfloat16),
             pltpu.VMEM((HALO, TOK, 128), jnp.bfloat16),
             pltpu.VMEM((HALO, TOK, 128), jnp.bfloat16),

time: 32.9 us -> 32.9 us (level)
  no operation moved by 1% of the time
where the time goes in v6:
time: 32.9 us; the launch traced here: 32.8 us
  Pallas kernels  32.1 us (98%)
  between operations  0.64 us (2%)
    pallas_call x1, Pallas kernels, per_device(): pl.pallas_call(functools.partial(kernel, depth), out_shape=pltpu.VMEM((2,...  31.2 us
    pallas_call x1, Pallas kernels, unpacked(): pl.pallas_call(unpack_kernel, out_shape=(jax.ShapeDtypeStruct(shape, jnp....  0.96 us

profile of v6, /device:TPU:224, one launch (start us, length us, event | category | flops | bytes accessed | tf_op | source)
XLA Modules:
  0.0 32.8 jit_solution(16878430814491969950)
XLA Ops:
  0.6 31.2 %shard_map.84.taken = bf16[2,16,2,32,128]{4,3,2,1,0:T(8,128)(2,1)S(1)} custom-call(bf16[2,32,1024]{2,1,0:T(8,128)(2,1)} %q_hbm.1, bf16[2,32,1024]{2,1,0:T(8,128)(2,1)} %k_hbm.1, bf16[2,32,1024]{2,1,0:T(8,128)(2,1)} %v_hbm.1, bf16[2,32,1024]{2,1,0:T(8,128)(2,1)} %g_hbm.1, s32[6,256]{1,0:T(8,128)} %bitcast.1), custom_call_target="tpu_custom_call" | custom-call | tf_op jit(solution)/shard_map/pallas_call | solution.py:494
  31.8 1.0 %shard_map.85 = (bf16[2,32,1024]{2,1,0:T(8,128)(2,1)}, bf16[2,32,1024]{2,1,0:T(8,128)(2,1)}, bf16[2,32,1024]{2,1,0:T(8,128)(2,1)}, bf16[2,32,1024]{2,1,0:T(8,128)(2,1)}) custom-call(bf16[2,16,2,32,128]{4,3,2,1,0:T(8,128)(2,1)S(1)} %shard_map.84.taken), custom_call_target="tpu_custom_call" | custom-call | tf_op jit(solution)/shard_map/pallas_call | solution.py:51
